TPU v7x, 128 devices: a whole 4x4x4 slice. The times are simulated.
128 devices in a mesh: grp: 2 (over core), dev: 64 (over z, x, y).
Axes of the slice: x: 4, y: 4, z: 4, core: 2. Of those that a mesh axis runs over, the one named last changes fastest.
Arguments:
- tokens: bfloat16 [32768, 2048], P(('grp', 'dev')), may hold values from -6 to 6
- modulation: float32 [128, 12288], P(('grp', 'dev')), may hold values from -3 to 3
- w_query: bfloat16 [2048, 1024], P(('grp', 'dev')), may hold values from -1 to 1
- w_key: bfloat16 [2048, 1024], P(('grp', 'dev')), may hold values from -1 to 1
- w_value: bfloat16 [2048, 1024], P(('grp', 'dev')), may hold values from -0.125 to 0.125
- w_out: bfloat16 [1024, 2048], P(None, ('grp', 'dev')), may hold values from -0.1875 to 0.1875
- w_in: bfloat16 [64, 2048, 4096], P('dev', None, 'grp'), may hold values from -0.125 to 0.125
- w_back: bfloat16 [64, 4096, 2048], P('dev', 'grp'), may hold values from -0.09375 to 0.09375
- routes: int32 [32768, 2], P(('grp', 'dev')), may hold values from 0 to 63, all different within a row; in each aligned block of 256 rows (0 to 255, 256 to 511, ...) at most 10 rows name the same one
- route_prob: float32 [32768, 2], P(('grp', 'dev')), may hold values from 0.2 to 1
Outputs:
- block_out: bfloat16 [32768, 2048], P(('grp', 'dev'))
Inputs may be any that keep to these rules, and one draw needn't show every extreme that they name: `routes`: the 2 experts of a token differ. Among the 256 tokens of one device (aligned blocks of rows), no expert is named more than 10 times, a bound that some block reaches.
All inputs are finite; a program needn't handle non-finite values.
Results may differ from a plain program's by a relative error of at most 0.0055.
Values may be sent and summed in bfloat16 or wider, within the bound.
No kernel may reach another device: no remote copies, remote signals or barrier semaphores. Data moves between devices by JAX's collectives and lax.ppermute only.
A program may use at most 128 MiB of HBM per device.

v0:
```python
import functools

import jax
import jax.numpy as jnp
from jax import lax
from jax.experimental import pallas as pl
from jax.experimental.pallas import tpu as pltpu
from jax.sharding import PartitionSpec as P

HEADS = 8
HDIM = 128
TOP = 2
CAP = 10
PAIRS = (5,)
BF16 = jnp.bfloat16
F32 = jnp.float32
VMEM_LIMIT = 58 * 1024 * 1024


def mm(a, b):
    return jnp.dot(a, b, preferred_element_type=F32)


def normalize(values):
    row_mean = jnp.mean(values, axis=-1, keepdims=True)
    centered = values - row_mean
    variance = jnp.mean(centered * centered, axis=-1, keepdims=True)
    return centered * lax.rsqrt(variance + 1e-06)


def fold_matrix(transposed):
    row = lax.broadcasted_iota(jnp.int32, (256, 256), 1 if transposed else 0)
    col = lax.broadcasted_iota(jnp.int32, (256, 256), 0 if transposed else 1)
    source = ((row // 2) % 4) * 64 + (row // 8) * 2 + row % 2
    return (source == col).astype(BF16)


def fold(rows, matrix):
    stacked = jnp.concatenate([rows[:, q * 512 : (q + 1) * 512] for q in range(4)], axis=0)
    return mm(matrix, stacked).astype(BF16)


def attention_kernel(pairs, xn, tok, mod, sel, wq, wk, wv, wo, after, *rest):
    sends, mixed = rest[:-1], rest[-1]
    step = pl.program_id(0)

    @pl.when(step < 4)
    def _():
        x = xn[...]
        q = mm(x, wq[...]).astype(BF16)
        k = mm(x, wk[...]).astype(BF16)
        v = mm(x, wv[...]).astype(BF16)
        outs = []
        for h in range(2):
            cut = slice(h * HDIM, (h + 1) * HDIM)
            scores = lax.dot_general(
                q[:, cut], k[:, cut], (((1,), (1,)), ((), ())), preferred_element_type=F32
            ) * HDIM ** (-0.5)
            exponent = jnp.exp(scores - jnp.max(scores, axis=-1, keepdims=True))
            weights = (exponent / jnp.sum(exponent, axis=-1, keepdims=True)).astype(BF16)
            outs.append(mm(weights, v[:, cut]).astype(BF16))
        mixed[:, pl.ds(pl.multiple_of(step * 256, 256), 256)] = jnp.concatenate(outs, axis=1)

    @pl.when(step >= 4)
    def _():
        at = pl.ds(pl.multiple_of((step - 4) * 512, 512), 512)
        projected = lax.dot_general(
            mixed[...], wo[...], (((1,), (1,)), ((), ())), preferred_element_type=F32
        )
        after[:, at] = tok[:, at].astype(F32) + mod[2:3, at] * projected

    @pl.when(step == 7)
    def _():
        normed = (normalize(after[...]) * (1.0 + mod[4:5, :]) + mod[3:4, :]).astype(BF16)
        matrix = fold_matrix(False)
        pair = 0
        for count, send in zip(pairs, sends):
            for j in range(count):
                rows = mm(sel[pair * 128 : (pair + 1) * 128, :], normed).astype(BF16)
                for g in range(2):
                    send[g * 256 : (g + 1) * 256, j * 512 : (j + 1) * 512] = fold(
                        rows[g * 64 : (g + 1) * 64, :], matrix
                    )
                pair += 1


def attention(pairs, xn, tok, mod, sel, weights):
    rows, width = xn.shape
    whole = lambda a: pl.BlockSpec(a.shape, lambda i: (0,) * a.ndim)
    part = lambda first: pl.BlockSpec((width, 256), lambda i: (0, first + jnp.minimum(i, 3)))
    shapes = [jax.ShapeDtypeStruct((rows, width), F32)]
    shapes += [jax.ShapeDtypeStruct((512, 512 * n), BF16) for n in pairs]
    return pl.pallas_call(
        functools.partial(attention_kernel, pairs),
        grid=(8,),
        in_specs=[
            whole(xn),
            whole(tok),
            whole(mod),
            whole(sel),
            part(0),
            part(4),
            part(8),
            pl.BlockSpec((512, 1024), lambda i: (jnp.maximum(i - 4, 0), 3)),
        ],
        out_specs=[whole(s) for s in shapes],
        out_shape=shapes,
        scratch_shapes=[pltpu.VMEM((rows, 1024), BF16)],
        compiler_params=pltpu.CompilerParams(vmem_limit_bytes=VMEM_LIMIT),
        cost_estimate=pl.CostEstimate(
            flops=7 * 10**9, transcendentals=10**6, bytes_accessed=24 * 10**6
        ),
        name="attention",
    )(xn, tok, mod, sel, weights, weights, weights, weights)


def expert_kernel(pairs, own, other, w_first, w_second, own_out, other_out, x, hidden, out):
    step = pl.program_id(0)
    blocks = [(src, j) for src in range(2) for j in range(pairs)]

    @pl.when(step == 0)
    def _():
        matrix = fold_matrix(True)
        for n, (src, j) in enumerate(blocks):
            ref = (own, other)[src]
            for g in range(2):
                flat = mm(matrix, ref[g * 256 : (g + 1) * 256, j * 512 : (j + 1) * 512]).astype(BF16)
                for q in range(4):
                    x[n * 128 + g * 64 : n * 128 + (g + 1) * 64, q * 512 : (q + 1) * 512] = flat[
                        q * 64 : (q + 1) * 64, :
                    ]

    @pl.when(step < 8)
    def _():
        at = pl.ds(pl.multiple_of(step * 256, 256), 256)
        product = mm(x[...], w_first[...])
        hidden[:, at] = jax.nn.gelu(product, approximate=True).astype(BF16)

    @pl.when(step >= 8)
    def _():
        at = pl.ds(pl.multiple_of((step - 8) * 256, 256), 256)
        out[:, at] = mm(hidden[...], w_second[...]).astype(BF16)

    @pl.when(step == 15)
    def _():
        matrix = fold_matrix(False)
        for n, (src, j) in enumerate(blocks):
            ref = (own_out, other_out)[src]
            for g in range(2):
                ref[g * 256 : (g + 1) * 256, j * 512 : (j + 1) * 512] = fold(
                    out[n * 128 + g * 64 : n * 128 + (g + 1) * 64, :], matrix
                )


def expert_half(pairs, own, other, w_first, w_second):
    width, half = w_first.shape
    rows = 256 * pairs
    whole = pl.BlockSpec(own.shape, lambda i: (0, 0))
    return pl.pallas_call(
        functools.partial(expert_kernel, pairs),
        grid=(16,),
        in_specs=[
            whole,
            whole,
            pl.BlockSpec((width, 256), lambda i: (0, jnp.minimum(i, 7))),
            pl.BlockSpec((half, 256), lambda i: (0, jnp.maximum(i - 8, 0))),
        ],
        out_specs=[whole, whole],
        out_shape=[jax.ShapeDtypeStruct(own.shape, BF16)] * 2,
        scratch_shapes=[
            pltpu.VMEM((rows, width), BF16),
            pltpu.VMEM((rows, half), BF16),
            pltpu.VMEM((rows, width), BF16),
        ],
        compiler_params=pltpu.CompilerParams(vmem_limit_bytes=VMEM_LIMIT),
        cost_estimate=pl.CostEstimate(
            flops=4 * rows * width * half,
            transcendentals=rows * half,
            bytes_accessed=4 * width * half + 8 * rows * width,
        ),
        name="experts",
    )(own, other, w_first, w_second)


def combine_kernel(pairs, after, mod, pick0, pick1, prob, *rest):
    backs, result, flat = rest[: len(pairs)], rest[-2], rest[-1]
    matrix = fold_matrix(True)
    pair = 0
    for count, back in zip(pairs, backs):
        for j in range(count):
            for g in range(2):
                rows = mm(matrix, back[g * 256 : (g + 1) * 256, j * 512 : (j + 1) * 512]).astype(BF16)
                for q in range(4):
                    top = pair * 128 + g * 64
                    flat[top : top + 64, q * 512 : (q + 1) * 512] = rows[q * 64 : (q + 1) * 64, :]
            pair += 1
    for q in range(4):
        cut = slice(q * 512, (q + 1) * 512)
        mix = prob[:, 0:1] * mm(pick0[...], flat[:, cut]) + prob[:, 1:2] * mm(pick1[...], flat[:, cut])
        result[:, cut] = (after[:, cut] + mod[5:6, cut] * mix).astype(BF16)


def combine(pairs, after, mod, pick0, pick1, prob, backs):
    rows, width = after.shape
    vmem = pl.BlockSpec(memory_space=pltpu.VMEM)
    return pl.pallas_call(
        functools.partial(combine_kernel, pairs),
        in_specs=[vmem] * (5 + len(backs)),
        out_specs=vmem,
        out_shape=jax.ShapeDtypeStruct((rows, width), BF16),
        scratch_shapes=[pltpu.VMEM((128 * sum(pairs), width), BF16)],
        compiler_params=pltpu.CompilerParams(vmem_limit_bytes=VMEM_LIMIT),
        cost_estimate=pl.CostEstimate(
            flops=3 * 10**9, transcendentals=0, bytes_accessed=7 * 10**6
        ),
        name="combine",
    )(after, mod, pick0, pick1, prob, *backs)


def slots_of(routes, experts):
    tokens = routes.shape[0]
    ids = jnp.arange(experts, dtype=jnp.int32)
    chosen = [(routes[:, k : k + 1] == ids[None, :]) for k in range(TOP)]
    taken = sum(c.astype(BF16) for c in chosen)
    order = jnp.arange(tokens, dtype=jnp.int32)
    earlier = (order[:, None] > order[None, :]).astype(BF16)
    before = mm(earlier, taken)
    slots = []
    for k in range(TOP):
        rank = jnp.sum(jnp.where(chosen[k], before, 0.0), axis=1).astype(jnp.int32)
        slots.append((rank // 2) * (2 * experts) + routes[:, k] * 2 + rank % 2)
    return slots


def body(tokens, modulation, w_query, w_key, w_value, w_out, w_in, w_back, routes, route_prob):
    tok_rows, width = tokens.shape
    mod = modulation.reshape(6, width)
    pieces = jnp.concatenate([w_query, w_key, w_value, w_out.T], axis=1)
    weights = lax.all_gather(pieces, ("grp", "dev"), axis=0, tiled=True)

    xn = (normalize(tokens.astype(F32)) * (1.0 + mod[1:2]) + mod[0:1]).astype(BF16)
    experts = lax.axis_size("dev")
    rows = experts * CAP
    slots = slots_of(routes, experts)
    ids = jnp.arange(rows, dtype=jnp.int32)
    sel = sum((ids[:, None] == s[None, :]).astype(BF16) for s in slots)
    picks = [(s[:, None] == ids[None, :]).astype(BF16) for s in slots]

    after, *sends = attention(PAIRS, xn, tokens, mod, sel, weights)
    swap = [(0, 1), (1, 0)]
    backs = []
    for count, send in zip(PAIRS, sends):
        send = send.reshape(experts, 8, 512 * count)
        own = lax.all_to_all(send, "dev", split_axis=0, concat_axis=0, tiled=True)
        own = own.reshape(512, 512 * count)
        other = lax.ppermute(own, "grp", swap)
        own_out, other_out = expert_half(count, own, other, w_in[0], w_back[0])
        arrived = lax.ppermute(other_out, "grp", swap)
        total = (own_out.astype(F32) + arrived.astype(F32)).astype(BF16)
        total = total.reshape(experts, 8, 512 * count)
        back = lax.all_to_all(total, "dev", split_axis=0, concat_axis=0, tiled=True)
        backs.append(back.reshape(512, 512 * count))
    return combine(PAIRS, after, mod, picks[0], picks[1], route_prob, backs)


def solution(mesh):
    in_specs = (
        P(("grp", "dev"), None),
        P(("grp", "dev"), None),
        P(("grp", "dev"), None),
        P(("grp", "dev"), None),
        P(("grp", "dev"), None),
        P(None, ("grp", "dev")),
        P("dev", None, "grp"),
        P("dev", "grp", None),
        P(("grp", "dev"), None),
        P(("grp", "dev"), None),
    )
    out_specs = P(("grp", "dev"), None)
    return jax.shard_map(body, mesh=mesh, in_specs=in_specs, out_specs=out_specs, check_vma=False)
```

profile of v0, /device:TPU:0, one launch (start us, length us, event | category | flops | bytes accessed | tf_op | source)
XLA Modules:
  0.0 263.7 jit_solution(14347829764778246366)
XLA Ops:
  6.5 1.6 pad_maximum_fusion
  8.1 0.5 broadcast.333
  8.6 1.6 reduce.3
  10.2 0.6 reshape.261.mod
  10.8 0.8 fusion.24
  11.8 1.4 convert_reduce_fusion
  13.3 0.4 fusion.3
  13.7 0.9 fusion.11.sel
  14.7 0.7 slice_add_fusion
  15.4 1.4 fusion.6.xn
  16.8 76.5 %all-gather.2.cloned.1.call-done.wq.wk.wv.wo = bf16[2048,4096]{1,0:T(8,128)(2,1)} async-done(((bf16[16,4096]{1,0:T(8,128)(2,1)}), bf16[2048,4096]{1,0:T(8,128)(2,1)}) %all-gather.2.cloned.1.call-update) | async-done | bytes 16777232 | tf_op jit(solution)/shard_map/all_gather | solution.py:239
  93.3 18.9 %attention.1 = (f32[256,2048]{1,0:T(8,128)}, bf16[512,2560]{1,0:T(8,128)(2,1)}) custom-call(bf16[256,2048]{1,0:T(8,128)(2,1)} %fusion.6.xn, bf16[256,2048]{1,0:T(8,128)(2,1)} %tok.1, f32[6,2048]{1,0:T(8,128)} %reshape.261.mod, bf16[640,256]{1,0:T(8,128)(2,1)} %fusion.11.sel, bf16[2048,4096]{1,0:T(8,128)(2,1)} %all-gather.2.cloned.1.call-done.wq.wk.wv.wo, ...), custom_call_target="tpu_custom_call" | custom-call | flops 7000000000 | bytes 24000000 | tf_op jit(solution)/shard_map/attention/pallas_call | solution.py:93
  112.3 44.7 %all_to_all.10 = bf16[64,8,2560]{2,1,0:T(8,128)(2,1)S(1)} all-to-all(bf16[64,8,2560]{2,1,0:T(8,128)(2,1)} %bitcast.19), channel_id=1, replica_groups=mesh['grp'=2,'dev'=64] {'dev'}, dimensions={0} | all-to-all | bytes 5242880 | tf_op jit(solution)/shard_map/all_to_all | solution.py:254
  157.0 4.9 %collective-permute-done.other = bf16[512,2560]{1,0:T(8,128)(2,1)S(1)} collective-permute-done((bf16[512,2560]{1,0:T(8,128)(2,1)S(1)}, bf16[512,2560]{1,0:T(8,128)(2,1)S(1)}, u32[]{:S(2)}, u32[]{:S(2)}) %collective-permute-start) | collective-permute-done | bytes 2621472 | tf_op jit(solution)/shard_map/ppermute | solution.py:256
  161.9 1.5 copy-done.5
  163.4 35.5 %experts.1 = (bf16[512,2560]{1,0:T(8,128)(2,1)}, bf16[512,2560]{1,0:T(8,128)(2,1)}) custom-call(bf16[512,2560]{1,0:T(8,128)(2,1)} %bitcast.18, bf16[512,2560]{1,0:T(8,128)(2,1)} %copy-done.5, bf16[2048,2048]{1,0:T(8,128)(2,1)} %bitcast.31, bf16[2048,2048]{1,0:T(8,128)(2,1)} %bitcast.32), custom_call_target="tpu_custom_call" | custom-call | flops 21474836480 | bytes 37748736 | tf_op jit(solution)/shard_map/experts/pallas_call | solution.py:159
  199.0 5.0 %collective-permute-done.1 = bf16[512,2560]{1,0:T(8,128)(2,1)S(1)} collective-permute-done((bf16[512,2560]{1,0:T(8,128)(2,1)}, bf16[512,2560]{1,0:T(8,128)(2,1)S(1)}, u32[]{:S(2)}, u32[]{:S(2)}) %collective-permute-start.1) | collective-permute-done | bytes 2621472 | tf_op jit(solution)/shard_map/ppermute | solution.py:258
  204.0 3.9 %fusion = bf16[64,8,2560]{2,1,0:T(8,128)(2,1)} fusion(bf16[512,2560]{1,0:T(8,128)(2,1)S(1)} %collective-permute-done.1, bf16[512,2560]{1,0:T(8,128)(2,1)} %get-tuple-element.11), kind=kLoop, calls=%fused_computation.3 | loop fusion | flops 5242880 | bytes 7864320 | tf_op jit(solution)/shard_map/reshape | solution.py:260
  207.9 5.6 %all-to-all-start.1 = ((bf16[64,8,2560]{2,1,0:T(8,128)(2,1)}), bf16[64,8,2560]{2,1,0:T(8,128)(2,1)S(1)}, u32[]{:S(2)}, u32[]{:S(2)}) async-start(bf16[64,8,2560]{2,1,0:T(8,128)(2,1)} %fusion), calls=%async_computation.1 | async-start | bytes 5242880 | tf_op jit(solution)/shard_map/all_to_all | solution.py:261
  213.6 0.8 copy.11.prob
  214.4 1.0 fusion.9
  215.4 33.7 %all-to-all-done.1 = bf16[64,8,2560]{2,1,0:T(8,128)(2,1)S(1)} async-done(((bf16[64,8,2560]{2,1,0:T(8,128)(2,1)}), bf16[64,8,2560]{2,1,0:T(8,128)(2,1)S(1)}, u32[]{:S(2)}, u32[]{:S(2)}) %all-to-all-start.1) | async-done | bytes 2621472 | tf_op jit(solution)/shard_map/all_to_all | solution.py:261
  249.1 1.5 copy-done.1
  250.6 6.2 %combine.1 = bf16[256,2048]{1,0:T(8,128)(2,1)} custom-call(f32[256,2048]{1,0:T(8,128)} %get-tuple-element.9.after, f32[6,2048]{1,0:T(8,128)} %reshape.261.mod, bf16[256,640]{1,0:T(8,128)(2,1)} %get-tuple-element.23.pick0, bf16[256,640]{1,0:T(8,128)(2,1)} %get-tuple-element.24.pick1, f32[256,2]{1,0:T(8,128)} %copy.11.prob, bf16[512,2560]{1,0:T(8,128)(2,1)} %bitcast.16), custom_call_target="tpu_custom_call" | custom-call | flops 3000000000 | bytes 7000000 | tf_op jit(solution)/shard_map/combine/pallas_call | solution.py:206
  (21 shorter events, 0.5 us)
Async XLA Ops:
  6.5 6.7 %copy-start = (bf16[256,2048]{1,0:T(8,128)(2,1)S(1)}, bf16[256,2048]{1,0:T(8,128)(2,1)}, u32[]{:S(2)}) copy-start(bf16[256,2048]{1,0:T(8,128)(2,1)} %tok.1) | copy-start | bytes 3145732
  6.5 86.8 %all-gather.2.cloned.1.call-start = ((), (), s32[]{:S(2)}) async-start(), calls=%async_computation.2 | async-start | bytes 16908288 | tf_op jit(solution)/shard_map/all_gather | solution.py:239
  157.0 4.9 %copy-start.2 = (bf16[64,8,2560]{2,1,0:T(8,128)(2,1)}, bf16[64,8,2560]{2,1,0:T(8,128)(2,1)S(1)}, u32[]{:S(2)}) copy-start(bf16[64,8,2560]{2,1,0:T(8,128)(2,1)S(1)} %all_to_all.10) | copy-start | bytes 7864324
  157.0 4.9 %collective-permute-start = (bf16[512,2560]{1,0:T(8,128)(2,1)S(1)}, bf16[512,2560]{1,0:T(8,128)(2,1)S(1)}, u32[]{:S(2)}, u32[]{:S(2)}) collective-permute-start(bf16[512,2560]{1,0:T(8,128)(2,1)S(1)} %bitcast.17), channel_id=1, source_target_pairs={{0,64},{64,0},{1,65},{65,1},{2,66},{66,2},{3,67},{67,3},{4,68},{68... | collective-permute-start | bytes 7864328 | tf_op jit(solution)/shard_map/ppermute | solution.py:256
  161.9 1.5 copy-start.5
  198.9 5.1 %collective-permute-start.1 = (bf16[512,2560]{1,0:T(8,128)(2,1)}, bf16[512,2560]{1,0:T(8,128)(2,1)S(1)}, u32[]{:S(2)}, u32[]{:S(2)}) collective-permute-start(bf16[512,2560]{1,0:T(8,128)(2,1)} %get-tuple-element.12), channel_id=1, source_target_pairs={{0,64},{64,0},{1,65},{65,1},{2,66},{66,2},{3,67},{67,3},{4,68},{68... | collective-permute-start | bytes 7864328 | tf_op jit(solution)/shard_map/ppermute | solution.py:258
  207.9 5.6 %copy-start.4 = (f32[256,2]{0,1:T(2,128)S(1)}, f32[256,2]{0,1:T(2,128)}, u32[]{:S(2)}) copy-start(f32[256,2]{0,1:T(2,128)} %param.19) | copy-start | bytes 6148
  207.9 6.5 %copy-start.3 = (s32[256,2]{0,1:T(2,128)S(1)}, s32[256,2]{0,1:T(2,128)}, u32[]{:S(2)}) copy-start(s32[256,2]{0,1:T(2,128)} %param.18) | copy-start | bytes 6148
  207.9 41.2 %all-to-all-start.1 = ((bf16[64,8,2560]{2,1,0:T(8,128)(2,1)}), bf16[64,8,2560]{2,1,0:T(8,128)(2,1)S(1)}, u32[]{:S(2)}, u32[]{:S(2)}) async-start(bf16[64,8,2560]{2,1,0:T(8,128)(2,1)} %fusion), calls=%async_computation.1 | async-start | bytes 5242880 | tf_op jit(solution)/shard_map/all_to_all | solution.py:261
  249.1 1.5 copy-start.1
Sparse Core Ops, SparseCore 0:
  10.5 82.7 all-gather.1
where the time goes:
time: 264 us
  waiting for transfers between devices  120 us (45%)
  Pallas kernels  60.7 us (23%)
  blocking collectives  44.7 us (17%)
  between operations  13.5 us (5%)
  other arithmetic  13.1 us (5%)
  starting transfers between devices  5.75 us (2%)
  local copies, waits for them, and re-layouts  5.74 us (2%)
    all_gather x1, waiting for transfers between devices, body(): weights = lax.all_gather(pieces, ('grp', 'dev'), axis=0, tiled=True)  76.5 us
    all_to_all x1, blocking collectives, body(): own = lax.all_to_all(send, 'dev', split_axis=0, concat_axis=0, tiled=True)  44.7 us
    pallas_call x1, Pallas kernels, expert_half(): pl.pallas_call(functools.partial(expert_kernel, pairs), grid=(16,), in_sp...  35.5 us
    all_to_all x1, waiting for transfers between devices, body(): back = lax.all_to_all(total, 'dev', split_axis=0, concat_axis=0, tiled=True)  33.7 us
    pallas_call x1, Pallas kernels, attention(): pl.pallas_call(functools.partial(attention_kernel, pairs), grid=(8,), in_...  18.9 us
    pallas_call x1, Pallas kernels, combine(): pl.pallas_call(functools.partial(combine_kernel, pairs), in_specs=[vmem]...  6.2 us
    all_to_all x1, starting transfers between devices, body(): back = lax.all_to_all(total, 'dev', split_axis=0, concat_axis=0, tiled=True)  5.61 us
  transfers between devices with their start and end apart: 4, of which 4 were waited for; matrix products, arithmetic and copies ran while one was open for 4% of the time, Pallas kernels for 0%

commit v1 on v0

v1 whole, which is shorter than its diff:
```python
import jax
import jax.numpy as jnp
from jax import lax
from jax.experimental import pallas as pl
from jax.experimental.pallas import tpu as pltpu
from jax.sharding import PartitionSpec as P

HEADS = 8
HDIM = 128
TOP = 2
CAP = 10
PAIRS = (3, 2)
TILE = 512
WIDE = 1024
TALL = 2048
MB = 256
BF16 = jnp.bfloat16
F32 = jnp.float32
MIB = 1024 * 1024


def mm(a, b):
    return jnp.dot(a, b, preferred_element_type=F32)


def in_hbm(array):
    return pltpu.with_memory_space_constraint(array, pltpu.HBM)


def normalize(values):
    row_mean = jnp.mean(values, axis=-1, keepdims=True)
    centered = values - row_mean
    variance = jnp.mean(centered * centered, axis=-1, keepdims=True)
    return centered * lax.rsqrt(variance + 1e-06)


def fold_matrix(transposed):
    row = lax.broadcasted_iota(jnp.int32, (256, 256), 1 if transposed else 0)
    col = lax.broadcasted_iota(jnp.int32, (256, 256), 0 if transposed else 1)
    source = ((row // 2) % 4) * 64 + (row // 8) * 2 + row % 2
    return (source == col).astype(BF16)


def fold(rows, matrix):
    stacked = jnp.concatenate([rows[:, q * 512 : (q + 1) * 512] for q in range(4)], axis=0)
    return mm(matrix, stacked).astype(BF16)


def attention_kernel(xn, tok, mod, sel, weights, after_out, *rest):
    sends, (after, mixed, held, sems) = rest[: len(PAIRS)], rest[len(PAIRS) :]
    width, inner = xn.shape[1], mixed.shape[1]
    groups = inner // WIDE
    copies = []

    def fetch(rows, cols):
        copies.append(
            pltpu.make_async_copy(weights.at[rows, cols], held.at[rows, cols], sems.at[len(copies)])
        )
        copies[-1].start()

    for n in range(groups):
        for part in range(3):
            fetch(pl.ds(0, width), pl.ds(part * inner + n * WIDE, WIDE))
    for n in range(width // TALL):
        fetch(pl.ds(n * TALL, TALL), pl.ds(3 * inner, inner))

    for n in range(groups):
        projections = []
        for part in range(3):
            copies[3 * n + part].wait()
            first = part * inner + n * WIDE
            projections.append(mm(xn[...], held[:, first : first + WIDE]).astype(BF16))
        q, k, v = projections
        for h in range(WIDE // HDIM):
            cut = slice(h * HDIM, (h + 1) * HDIM)
            scores = lax.dot_general(
                q[:, cut], k[:, cut], (((1,), (1,)), ((), ())), preferred_element_type=F32
            ) * HDIM ** (-0.5)
            exponent = jnp.exp(scores - jnp.max(scores, axis=-1, keepdims=True))
            attn = (exponent / jnp.sum(exponent, axis=-1, keepdims=True)).astype(BF16)
            mixed[:, n * WIDE + h * HDIM : n * WIDE + (h + 1) * HDIM] = mm(attn, v[:, cut]).astype(BF16)

    for n in range(width // TALL):
        copies[3 * groups + n].wait()
        cut = slice(n * TALL, (n + 1) * TALL)
        projected = lax.dot_general(
            mixed[...], held[cut, 3 * inner :], (((1,), (1,)), ((), ())), preferred_element_type=F32
        )
        after[:, cut] = tok[:, cut].astype(F32) + mod[2:3, cut] * projected

    keep = pltpu.make_async_copy(after, after_out, sems.at[len(copies)])
    keep.start()
    normed = (normalize(after[...]) * (1.0 + mod[4:5, :]) + mod[3:4, :]).astype(BF16)
    matrix = fold_matrix(False)
    pair = 0
    for send in sends:
        for j in range(send.shape[1] // 512):
            rows = mm(sel[pair * 128 : (pair + 1) * 128, :], normed).astype(BF16)
            for g in range(2):
                send[g * 256 : (g + 1) * 256, j * 512 : (j + 1) * 512] = fold(
                    rows[g * 64 : (g + 1) * 64, :], matrix
                )
            pair += 1
    keep.wait()


def attention(xn, tok, mod, sel, weights):
    rows, width = xn.shape
    inner = HEADS * HDIM
    vmem = pl.BlockSpec(memory_space=pltpu.VMEM)
    return pl.pallas_call(
        attention_kernel,
        in_specs=[vmem] * 4 + [pl.BlockSpec(memory_space=pltpu.HBM)],
        out_specs=[pl.BlockSpec(memory_space=pltpu.HBM)] + [vmem] * len(PAIRS),
        out_shape=[pltpu.HBM((rows, width), F32)]
        + [jax.ShapeDtypeStruct((512, 512 * n), BF16) for n in PAIRS],
        scratch_shapes=[
            pltpu.VMEM((rows, width), F32),
            pltpu.VMEM((rows, inner), BF16),
            pltpu.VMEM((width, 4 * inner), BF16),
            pltpu.SemaphoreType.DMA((3 * (inner // WIDE) + width // TALL + 1,)),
        ],
        compiler_params=pltpu.CompilerParams(vmem_limit_bytes=48 * MIB),
        cost_estimate=pl.CostEstimate(
            flops=7 * 10**9, transcendentals=10**6, bytes_accessed=24 * 10**6
        ),
        name="attention",
    )(xn, tok, mod, sel, in_hbm(weights))


def expert_kernel(own, other, w_first, w_second, own_out, other_out, x, hidden, first, second, sems):
    pairs = own.shape[1] // 512
    tiles = first.shape[1] // TILE
    blocks = [(src, j) for src in range(2) for j in range(pairs)]

    def fetch(which, n):
        source, target = ((w_first, first), (w_second, second))[which]
        cut = pl.ds(pl.multiple_of(n * TILE, TILE), TILE)
        return pltpu.make_async_copy(
            source.at[:, cut], target.at[:, cut], sems.at[which * tiles + n]
        )

    for which in range(2):
        for n in range(tiles):
            fetch(which, n).start()

    matrix = fold_matrix(True)
    for n, (src, j) in enumerate(blocks):
        ref = (own, other)[src]
        for g in range(2):
            flat = mm(matrix, ref[g * 256 : (g + 1) * 256, j * 512 : (j + 1) * 512]).astype(BF16)
            for q in range(4):
                x[n * 128 + g * 64 : n * 128 + (g + 1) * 64, q * 512 : (q + 1) * 512] = flat[
                    q * 64 : (q + 1) * 64, :
                ]

    @pl.loop(0, tiles)
    def _(n):
        fetch(0, n).wait()
        cut = pl.ds(pl.multiple_of(n * TILE, TILE), TILE)
        for m in range(0, x.shape[0], MB):
            product = mm(x[m : m + MB, :], first[:, cut])
            hidden[m : m + MB, cut] = jax.nn.gelu(product, approximate=True).astype(BF16)

    @pl.loop(0, tiles)
    def _(n):
        fetch(1, n).wait()
        cut = pl.ds(pl.multiple_of(n * TILE, TILE), TILE)
        for m in range(0, x.shape[0], MB):
            x[m : m + MB, cut] = mm(hidden[m : m + MB, :], second[:, cut]).astype(BF16)

    matrix = fold_matrix(False)
    for n, (src, j) in enumerate(blocks):
        ref = (own_out, other_out)[src]
        for g in range(2):
            ref[g * 256 : (g + 1) * 256, j * 512 : (j + 1) * 512] = fold(
                x[n * 128 + g * 64 : n * 128 + (g + 1) * 64, :], matrix
            )


def expert_half(own, other, w_first, w_second):
    width, half = w_first.shape
    rows = own.shape[1] // 2
    vmem = pl.BlockSpec(memory_space=pltpu.VMEM)
    hbm = pl.BlockSpec(memory_space=pltpu.HBM)
    return pl.pallas_call(
        expert_kernel,
        in_specs=[vmem, vmem, hbm, hbm],
        out_specs=[vmem, vmem],
        out_shape=[jax.ShapeDtypeStruct(own.shape, BF16)] * 2,
        scratch_shapes=[
            pltpu.VMEM((rows, width), BF16),
            pltpu.VMEM((rows, half), BF16),
            pltpu.VMEM((width, half), BF16),
            pltpu.VMEM((half, width), BF16),
            pltpu.SemaphoreType.DMA((2 * (half // TILE),)),
        ],
        compiler_params=pltpu.CompilerParams(vmem_limit_bytes=36 * MIB),
        cost_estimate=pl.CostEstimate(
            flops=4 * rows * width * half,
            transcendentals=rows * half,
            bytes_accessed=4 * width * half + 8 * rows * width,
        ),
        name="experts",
    )(own, other, in_hbm(w_first), in_hbm(w_second))


def combine_kernel(after_out, mod, pick0, pick1, prob, *rest):
    backs, (result, after, flat, sem) = rest[: len(PAIRS)], rest[len(PAIRS) :]
    kept = pltpu.make_async_copy(after_out, after, sem)
    kept.start()
    matrix = fold_matrix(True)
    top = 0
    for back in backs:
        for j in range(back.shape[1] // 512):
            for g in range(2):
                rows = mm(matrix, back[g * 256 : (g + 1) * 256, j * 512 : (j + 1) * 512]).astype(BF16)
                for q in range(4):
                    flat[top : top + 64, q * 512 : (q + 1) * 512] = rows[q * 64 : (q + 1) * 64, :]
                top += 64
    kept.wait()
    for q in range(4):
        cut = slice(q * 512, (q + 1) * 512)
        mix = prob[:, 0:1] * mm(pick0[...], flat[:, cut]) + prob[:, 1:2] * mm(pick1[...], flat[:, cut])
        result[:, cut] = (after[:, cut] + mod[5:6, cut] * mix).astype(BF16)


def combine(after, mod, pick0, pick1, prob, backs):
    rows, width = after.shape
    vmem = pl.BlockSpec(memory_space=pltpu.VMEM)
    return pl.pallas_call(
        combine_kernel,
        in_specs=[pl.BlockSpec(memory_space=pltpu.HBM)] + [vmem] * (4 + len(backs)),
        out_specs=vmem,
        out_shape=jax.ShapeDtypeStruct((rows, width), BF16),
        scratch_shapes=[
            pltpu.VMEM((rows, width), F32),
            pltpu.VMEM((128 * sum(PAIRS), width), BF16),
            pltpu.SemaphoreType.DMA,
        ],
        compiler_params=pltpu.CompilerParams(vmem_limit_bytes=16 * MIB),
        cost_estimate=pl.CostEstimate(
            flops=3 * 10**9, transcendentals=0, bytes_accessed=7 * 10**6
        ),
        name="combine",
    )(in_hbm(after), mod, pick0, pick1, prob, *backs)


def diagonal_order(experts):
    return sorted(range(experts), key=diagonal_place)


def diagonal_place(chip):
    z, x, y = chip // 16, (chip // 4) % 4, chip % 4
    return (y - z) % 4 * 16 + (x - z) % 4 * 4 + z


def slots_of(routes, experts):
    tokens = routes.shape[0]
    routes = diagonal_place(routes)
    ids = jnp.arange(experts, dtype=jnp.int32)
    chosen = [(routes[:, k : k + 1] == ids[None, :]) for k in range(TOP)]
    taken = sum(c.astype(BF16) for c in chosen)
    order = jnp.arange(tokens, dtype=jnp.int32)
    earlier = (order[:, None] > order[None, :]).astype(BF16)
    before = mm(earlier, taken)
    slots = []
    for k in range(TOP):
        rank = jnp.sum(jnp.where(chosen[k], before, 0.0), axis=1).astype(jnp.int32)
        slots.append((rank // 2) * (2 * experts) + routes[:, k] * 2 + rank % 2)
    return slots


def body(tokens, modulation, w_query, w_key, w_value, w_out, w_in, w_back, routes, route_prob):
    tok_rows, width = tokens.shape
    mod = modulation.reshape(6, width)
    pieces = jnp.concatenate([w_query, w_key, w_value, w_out.T], axis=1)
    weights = lax.all_gather(pieces, ("grp", "dev"), axis=0, tiled=True)

    xn = (normalize(tokens.astype(F32)) * (1.0 + mod[1:2]) + mod[0:1]).astype(BF16)
    experts = lax.axis_size("dev")
    rows = experts * CAP
    slots = slots_of(routes, experts)
    ids = jnp.arange(rows, dtype=jnp.int32)
    sel = sum((ids[:, None] == s[None, :]).astype(BF16) for s in slots)
    picks = [(s[:, None] == ids[None, :]).astype(BF16) for s in slots]

    after, *sends = attention(xn, tokens, mod, sel, weights)
    swap = [(0, 1), (1, 0)]

    def shuffle(rows):
        folded = rows.reshape(experts, 8, -1)
        groups = [diagonal_order(experts)]
        return lax.all_to_all(
            folded, "dev", split_axis=0, concat_axis=0, tiled=True, axis_index_groups=groups
        ).reshape(rows.shape)

    add = lambda a, b: (a.astype(F32) + b.astype(F32)).astype(BF16)
    w_first, w_second = w_in[0], w_back[0]

    own_a, own_b = [shuffle(send) for send in sends]
    mine_a, theirs_a = expert_half(own_a, lax.ppermute(own_a, "grp", swap), w_first, w_second)
    own_b, theirs_a = lax.optimization_barrier((own_b, theirs_a))
    other_b = lax.ppermute(own_b, "grp", swap)
    total_a = add(mine_a, lax.ppermute(theirs_a, "grp", swap))
    total_a, other_b = lax.optimization_barrier((total_a, other_b))
    back_a = shuffle(total_a)
    mine_b, theirs_b = expert_half(own_b, other_b, w_first, w_second)
    back_a, theirs_b = lax.optimization_barrier((back_a, theirs_b))
    total_b = add(mine_b, lax.ppermute(theirs_b, "grp", swap))
    backs = [back_a, shuffle(total_b)]
    return combine(after, mod, picks[0], picks[1], route_prob, backs)


def solution(mesh):
    in_specs = (
        P(("grp", "dev"), None),
        P(("grp", "dev"), None),
        P(("grp", "dev"), None),
        P(("grp", "dev"), None),
        P(("grp", "dev"), None),
        P(None, ("grp", "dev")),
        P("dev", None, "grp"),
        P("dev", "grp", None),
        P(("grp", "dev"), None),
        P(("grp", "dev"), None),
    )
    out_specs = P(("grp", "dev"), None)
    return jax.shard_map(body, mesh=mesh, in_specs=in_specs, out_specs=out_specs, check_vma=False)
```

time: 264 us -> 248 us (0.939)
  starting transfers between devices: 5.75 us -> 24.2 us
  blocking collectives: 44.7 us -> 31.4 us
  waiting for transfers between devices: 120 us -> 108 us
  Pallas kernels: 60.7 us -> 52.5 us
  other arithmetic: 13.1 us -> 10.2 us
    all_to_all x1 -> x3, starting transfers between devices: 5.61 us -> 23.7 us  [shuffle(): lax.all_to_all(folded, 'dev', split_axis=0, concat_axis=0, tiled=True, ax...]
    all_to_all x1, blocking collectives: 44.7 us -> 31.4 us  [shuffle(): lax.all_to_all(folded, 'dev', split_axis=0, concat_axis=0, tiled=True, ax...]
    all_to_all x1 -> x3, waiting for transfers between devices: 33.7 us -> 22.9 us  [shuffle(): lax.all_to_all(folded, 'dev', split_axis=0, concat_axis=0, tiled=True, ax...]
    pallas_call x3 -> x4, Pallas kernels: 60.7 us -> 52.5 us  [the longest x2 34.3 us: expert_half(): pl.pallas_call(expert_kernel, in_specs=[vmem, vmem, hbm, hbm], out_specs=...]
    ppermute x2 -> x4, waiting for transfers between devices: 9.89 us -> 5.98 us  [the longest x1 3.11 us: body(): total_a = add(mine_a, lax.ppermute(theirs_a, 'grp', swap))]
    unnamed x14 -> x18, local copies, waits for them, and re-layouts: 4.34 us -> 7.55 us
  transfers between devices with their start and end apart: 4 -> 8, of which waited for: 4 -> 5; matrix products, arithmetic and copies ran while one was open for 4% -> 3% of each run, Pallas kernels for 0% -> 14%
where the time goes in v1:
time: 248 us
  waiting for transfers between devices  108 us (44%)
  Pallas kernels  52.5 us (21%)
  blocking collectives  31.4 us (13%)
  starting transfers between devices  24.2 us (10%)
  between operations  13.6 us (5%)
  other arithmetic  10.2 us (4%)
  local copies, waits for them, and re-layouts  7.56 us (3%)
    all_gather x1, waiting for transfers between devices, body(): weights = lax.all_gather(pieces, ('grp', 'dev'), axis=0, tiled=True)  78.9 us
    pallas_call x2, Pallas kernels, expert_half(): pl.pallas_call(expert_kernel, in_specs=[vmem, vmem, hbm, hbm], out_specs=...  34.3 us
    all_to_all x1, blocking collectives, shuffle(): lax.all_to_all(folded, 'dev', split_axis=0, concat_axis=0, tiled=True, ax...  31.4 us
    all_to_all x3, starting transfers between devices, shuffle(): lax.all_to_all(folded, 'dev', split_axis=0, concat_axis=0, tiled=True, ax...  23.7 us
    all_to_all x3, waiting for transfers between devices, shuffle(): lax.all_to_all(folded, 'dev', split_axis=0, concat_axis=0, tiled=True, ax...  22.9 us
    pallas_call x1, Pallas kernels, attention(): pl.pallas_call(attention_kernel, in_specs=[vmem] * 4 + [pl.BlockSpec(memo...  13.1 us
    unnamed x18, local copies, waits for them, and re-layouts  7.55 us
    pallas_call x1, Pallas kernels, combine(): pl.pallas_call(combine_kernel, in_specs=[pl.BlockSpec(memory_space=pltpu....  5.1 us
  transfers between devices with their start and end apart: 8, of which 5 were waited for; matrix products, arithmetic and copies ran while one was open for 3% of the time, Pallas kernels for 14%

profile of v1, /device:TPU:0, one launch (start us, length us, event | category | flops | bytes accessed | tf_op | source)
XLA Modules:
  0.0 247.5 jit_solution(3252991465643180450)
XLA Ops:
  6.5 1.6 pad_maximum_fusion
  8.7 1.5 reduce.3
  11.2 1.4 convert_reduce_fusion
  14.5 78.9 %all-gather.2.cloned.1.call-done.weights = bf16[2048,4096]{1,0:T(8,128)(2,1)} async-done(((bf16[16,4096]{1,0:T(8,128)(2,1)}), bf16[2048,4096]{1,0:T(8,128)(2,1)}) %all-gather.2.cloned.1.call-update) | async-done | bytes 16777232 | tf_op jit(solution)/shard_map/all_gather | solution.py:278
  93.3 13.1 %attention.1 = (f32[256,2048]{1,0:T(8,128)}, bf16[512,1536]{1,0:T(8,128)(2,1)S(1)}, bf16[512,1024]{1,0:T(8,128)(2,1)}) custom-call(bf16[256,2048]{1,0:T(8,128)(2,1)S(1)} %fusion.5.xn, bf16[256,2048]{1,0:T(8,128)(2,1)S(1)} %copy-done, f32[6,2048]{1,0:T(8,128)S(1)} %reshape.273.mod, bf16[640,256]{1,0:T(8,128)(2,1)S(1)} %fusion.11.sel, ...), custom_call_target="tpu_custom_call" | custom-call | flops 7000000000 | bytes 24000000 | tf_op jit(solution)/shard_map/attention/pallas_call | solution.py:111
  106.4 31.4 %all_to_all.20 = bf16[64,8,1536]{2,1,0:T(8,128)(2,1)S(1)} all-to-all(bf16[64,8,1536]{2,1,0:T(8,128)(2,1)S(1)} %bitcast.23), channel_id=1, replica_groups={{0,21,42,63,4,25,46,51,8,29,34,55,12,17,38,59,1,22,43,60,5,26,47,48,9,3..., dimensions={0} | all-to-all | bytes 3145728 | tf_op jit(solution)/shard_map/all_to_all | solution.py:294
  137.9 7.0 %all-to-all-start.1 = ((bf16[64,8,1024]{2,1,0:T(8,128)(2,1)}), bf16[64,8,1024]{2,1,0:T(8,128)(2,1)}, u32[]{:S(2)}, u32[]{:S(2)}) async-start(bf16[64,8,1024]{2,1,0:T(8,128)(2,1)} %bitcast.13), calls=%async_computation.1 | async-start | bytes 2097152 | tf_op jit(solution)/shard_map/all_to_all | solution.py:294
  144.9 1.2 copy-done.2
  146.1 1.4 copy-done.3
  147.5 19.2 %experts.2 = (bf16[512,1536]{1,0:T(8,128)(2,1)S(1)}, bf16[512,1536]{1,0:T(8,128)(2,1)S(1)}) custom-call(bf16[512,1536]{1,0:T(8,128)(2,1)S(1)} %bitcast.22, bf16[512,1536]{1,0:T(8,128)(2,1)S(1)} %copy-done.3, bf16[2048,2048]{1,0:T(8,128)(2,1)} %bitcast.37, bf16[2048,2048]{1,0:T(8,128)(2,1)} %bitcast.39), custom_call_target="tpu_custom_call" | custom-call | flops 12884901888 | bytes 29360128 | tf_op jit(solution)/shard_map/experts/pallas_call | solution.py:186
  166.7 1.2 copy-done.1
  168.4 3.1 %collective-permute-done.1 = bf16[512,1536]{1,0:T(8,128)(2,1)S(1)} collective-permute-done((bf16[512,1536]{1,0:T(8,128)(2,1)}, bf16[512,1536]{1,0:T(8,128)(2,1)S(1)}, u32[]{:S(2)}, u32[]{:S(2)}) %collective-permute-start.1) | collective-permute-done | bytes 1572896 | tf_op jit(solution)/shard_map/ppermute | solution.py:305
  171.5 1.5 add_convert_fusion
  173.1 1.0 copy-done.4
  174.0 10.0 %all-to-all-start.2 = ((bf16[64,8,1536]{2,1,0:T(8,128)(2,1)}), bf16[64,8,1536]{2,1,0:T(8,128)(2,1)S(1)}, u32[]{:S(2)}, u32[]{:S(2)}) async-start(bf16[64,8,1536]{2,1,0:T(8,128)(2,1)} %bitcast.25), calls=%async_computation.2 | async-start | bytes 3145728 | tf_op jit(solution)/shard_map/all_to_all | solution.py:294
  184.0 1.2 copy-done.5
  185.2 15.1 %experts.3 = (bf16[512,1024]{1,0:T(8,128)(2,1)S(1)}, bf16[512,1024]{1,0:T(8,128)(2,1)S(1)}) custom-call(bf16[512,1024]{1,0:T(8,128)(2,1)} %bitcast.14.own, bf16[512,1024]{1,0:T(8,128)(2,1)S(1)} %copy-done.5, bf16[2048,2048]{1,0:T(8,128)(2,1)} %bitcast.38, bf16[2048,2048]{1,0:T(8,128)(2,1)} %bitcast.40), custom_call_target="tpu_custom_call" | custom-call | flops 8589934592 | bytes 25165824 | tf_op jit(solution)/shard_map/experts/pallas_call | solution.py:186
  200.3 1.0 copy-done.6
  201.3 5.7 %all-to-all-done.2 = bf16[64,8,1536]{2,1,0:T(8,128)(2,1)S(1)} async-done(((bf16[64,8,1536]{2,1,0:T(8,128)(2,1)}), bf16[64,8,1536]{2,1,0:T(8,128)(2,1)S(1)}, u32[]{:S(2)}, u32[]{:S(2)}) %all-to-all-start.2) | async-done | bytes 1572896 | tf_op jit(solution)/shard_map/all_to_all | solution.py:294
  207.0 2.9 %collective-permute-done.3 = bf16[512,1024]{1,0:T(8,128)(2,1)S(1)} collective-permute-done((bf16[512,1024]{1,0:T(8,128)(2,1)}, bf16[512,1024]{1,0:T(8,128)(2,1)S(1)}, u32[]{:S(2)}, u32[]{:S(2)}) %collective-permute-start.3) | collective-permute-done | bytes 1048608 | tf_op jit(solution)/shard_map/ppermute | solution.py:310
  209.9 1.4 fusion.6
  211.3 6.7 %all-to-all-start.3 = ((bf16[64,8,1024]{2,1,0:T(8,128)(2,1)}), bf16[64,8,1024]{2,1,0:T(8,128)(2,1)S(1)}, u32[]{:S(2)}, u32[]{:S(2)}) async-start(bf16[64,8,1024]{2,1,0:T(8,128)(2,1)} %fusion.6), calls=%async_computation.3 | async-start | bytes 2097152 | tf_op jit(solution)/shard_map/all_to_all | solution.py:294
  218.4 17.2 %all-to-all-done.3 = bf16[64,8,1024]{2,1,0:T(8,128)(2,1)S(1)} async-done(((bf16[64,8,1024]{2,1,0:T(8,128)(2,1)}), bf16[64,8,1024]{2,1,0:T(8,128)(2,1)S(1)}, u32[]{:S(2)}, u32[]{:S(2)}) %all-to-all-start.3) | async-done | bytes 1048608 | tf_op jit(solution)/shard_map/all_to_all | solution.py:294
  235.5 5.1 %combine.1 = bf16[256,2048]{1,0:T(8,128)(2,1)} custom-call(f32[256,2048]{1,0:T(8,128)} %get-tuple-element.18.after_out, f32[6,2048]{1,0:T(8,128)S(1)} %reshape.273.mod, bf16[256,640]{1,0:T(8,128)(2,1)S(1)} %get-tuple-element.41.pick0, bf16[256,640]{1,0:T(8,128)(2,1)S(1)} %get-tuple-element.42.pick1, f32[256,2]{1,0:T(8,128)S(1)} %copy.11.prob, ...), custom_call_target="tpu_custom_call" | custom-call | flops 3000000000 | bytes 7000000 | tf_op jit(solution)/shard_map/combine/pallas_call | solution.py:231
  (36 shorter events, 4.2 us)
Async XLA Ops:
  6.5 6.1 %copy-start = (bf16[256,2048]{1,0:T(8,128)(2,1)S(1)}, bf16[256,2048]{1,0:T(8,128)(2,1)}, u32[]{:S(2)}) copy-start(bf16[256,2048]{1,0:T(8,128)(2,1)} %tok.1) | copy-start | bytes 3145732
  6.5 86.8 %all-gather.2.cloned.1.call-start = ((), (), s32[]{:S(2)}) async-start(), calls=%async_computation.4 | async-start | bytes 16908288 | tf_op jit(solution)/shard_map/all_gather | solution.py:278
  137.9 7.1 %collective-permute-start = (bf16[512,1536]{1,0:T(8,128)(2,1)S(1)}, bf16[512,1536]{1,0:T(8,128)(2,1)S(1)}, u32[]{:S(2)}, u32[]{:S(2)}) collective-permute-start(bf16[512,1536]{1,0:T(8,128)(2,1)S(1)} %bitcast.21), channel_id=1, source_target_pairs={{0,64},{64,0},{1,65},{65,1},{2,66},{66,2},{3,67},{67,3},{4,68},{68... | collective-permute-start | bytes 4718600 | tf_op jit(solution)/shard_map/ppermute | solution.py:302
  137.9 30.0 %all-to-all-start.1 = ((bf16[64,8,1024]{2,1,0:T(8,128)(2,1)}), bf16[64,8,1024]{2,1,0:T(8,128)(2,1)}, u32[]{:S(2)}, u32[]{:S(2)}) async-start(bf16[64,8,1024]{2,1,0:T(8,128)(2,1)} %bitcast.13), calls=%async_computation.1 | async-start | bytes 2097152 | tf_op jit(solution)/shard_map/all_to_all | solution.py:294
  144.9 1.2 copy-start.2
  146.1 1.4 copy-start.3
  166.7 1.2 copy-start.1
  167.9 3.6 %collective-permute-start.1 = (bf16[512,1536]{1,0:T(8,128)(2,1)}, bf16[512,1536]{1,0:T(8,128)(2,1)S(1)}, u32[]{:S(2)}, u32[]{:S(2)}) collective-permute-start(bf16[512,1536]{1,0:T(8,128)(2,1)} %copy-done.1), channel_id=1, source_target_pairs={{0,64},{64,0},{1,65},{65,1},{2,66},{66,2},{3,67},{67,3},{4,68},{68... | collective-permute-start | bytes 4718600 | tf_op jit(solution)/shard_map/ppermute | solution.py:305
  168.1 4.9 %collective-permute-start.2 = (bf16[512,1024]{1,0:T(8,128)(2,1)}, bf16[512,1024]{1,0:T(8,128)(2,1)S(1)}, u32[]{:S(2)}, u32[]{:S(2)}) collective-permute-start(bf16[512,1024]{1,0:T(8,128)(2,1)} %bitcast.14.own), channel_id=1, source_target_pairs={{0,64},{64,0},{1,65},{65,1},{2,66},{66,2},{3,67},{67,3},{4,68},{68... | collective-permute-start | bytes 3145736 | tf_op jit(solution)/shard_map/ppermute | solution.py:304
  173.1 1.0 copy-start.4
  174.0 33.0 %all-to-all-start.2 = ((bf16[64,8,1536]{2,1,0:T(8,128)(2,1)}), bf16[64,8,1536]{2,1,0:T(8,128)(2,1)S(1)}, u32[]{:S(2)}, u32[]{:S(2)}) async-start(bf16[64,8,1536]{2,1,0:T(8,128)(2,1)} %bitcast.25), calls=%async_computation.2 | async-start | bytes 3145728 | tf_op jit(solution)/shard_map/all_to_all | solution.py:294
  184.0 1.2 copy-start.5
  200.3 1.0 copy-start.6
  207.0 2.9 %collective-permute-start.3 = (bf16[512,1024]{1,0:T(8,128)(2,1)}, bf16[512,1024]{1,0:T(8,128)(2,1)S(1)}, u32[]{:S(2)}, u32[]{:S(2)}) collective-permute-start(bf16[512,1024]{1,0:T(8,128)(2,1)} %copy-done.6), channel_id=1, source_target_pairs={{0,64},{64,0},{1,65},{65,1},{2,66},{66,2},{3,67},{67,3},{4,68},{68... | collective-permute-start | bytes 3145736 | tf_op jit(solution)/shard_map/ppermute | solution.py:310
  209.9 8.1 %copy-start.7 = (f32[256,2]{0,1:T(2,128)S(1)}, f32[256,2]{0,1:T(2,128)}, u32[]{:S(2)}) copy-start(f32[256,2]{0,1:T(2,128)} %param.19) | copy-start | bytes 6148
  211.3 24.3 %all-to-all-start.3 = ((bf16[64,8,1024]{2,1,0:T(8,128)(2,1)}), bf16[64,8,1024]{2,1,0:T(8,128)(2,1)S(1)}, u32[]{:S(2)}, u32[]{:S(2)}) async-start(bf16[64,8,1024]{2,1,0:T(8,128)(2,1)} %fusion.6), calls=%async_computation.3 | async-start | bytes 2097152 | tf_op jit(solution)/shard_map/all_to_all | solution.py:294
Sparse Core Ops, SparseCore 0:
  10.5 82.7 all-gather.1

commit v2 on v1

--- a/solution.py
+++ b/solution.py
@@ -9,7 +9,7 @@
 HDIM = 128
 TOP = 2
 CAP = 10
-PAIRS = (3, 2)
+PAIRS = (2, 3)
 TILE = 512
 WIDE = 1024
 TALL = 2048
@@ -120,7 +120,7 @@
             pltpu.VMEM((width, 4 * inner), BF16),
             pltpu.SemaphoreType.DMA((3 * (inner // WIDE) + width // TALL + 1,)),
         ],
-        compiler_params=pltpu.CompilerParams(vmem_limit_bytes=48 * MIB),
+        compiler_params=pltpu.CompilerParams(vmem_limit_bytes=26 * MIB),
         cost_estimate=pl.CostEstimate(
             flops=7 * 10**9, transcendentals=10**6, bytes_accessed=24 * 10**6
         ),
@@ -195,7 +195,7 @@
             pltpu.VMEM((half, width), BF16),
             pltpu.SemaphoreType.DMA((2 * (half // TILE),)),
         ],
-        compiler_params=pltpu.CompilerParams(vmem_limit_bytes=36 * MIB),
+        compiler_params=pltpu.CompilerParams(vmem_limit_bytes=25 * MIB),
         cost_estimate=pl.CostEstimate(
             flops=4 * rows * width * half,
             transcendentals=rows * half,
@@ -300,11 +300,10 @@
 
     own_a, own_b = [shuffle(send) for send in sends]
     mine_a, theirs_a = expert_half(own_a, lax.ppermute(own_a, "grp", swap), w_first, w_second)
-    own_b, theirs_a = lax.optimization_barrier((own_b, theirs_a))
+    total_a = add(mine_a, lax.ppermute(theirs_a, "grp", swap))
+    own_b, total_a = lax.optimization_barrier((own_b, total_a))
+    back_a = shuffle(total_a)
     other_b = lax.ppermute(own_b, "grp", swap)
-    total_a = add(mine_a, lax.ppermute(theirs_a, "grp", swap))
-    total_a, other_b = lax.optimization_barrier((total_a, other_b))
-    back_a = shuffle(total_a)
     mine_b, theirs_b = expert_half(own_b, other_b, w_first, w_second)
     back_a, theirs_b = lax.optimization_barrier((back_a, theirs_b))
     total_b = add(mine_b, lax.ppermute(theirs_b, "grp", swap))

time: 248 us -> 244 us (0.984)
  blocking collectives: 31.4 us -> 26 us
  local copies, waits for them, and re-layouts: 7.56 us -> 4.46 us
  waiting for transfers between devices: 108 us -> 111 us
    all_to_all x1, blocking collectives: 31.4 us -> 26 us  [shuffle(): lax.all_to_all(folded, 'dev', split_axis=0, concat_axis=0, tiled=True, ax...]
    all_to_all x3, waiting for transfers between devices: 22.9 us -> 26.6 us  [shuffle(): lax.all_to_all(folded, 'dev', split_axis=0, concat_axis=0, tiled=True, ax...]
    unnamed x18 -> x12, local copies, waits for them, and re-layouts: 7.55 us -> 4.45 us
where the time goes in v2:
time: 244 us
  waiting for transfers between devices  111 us (45%)
  Pallas kernels  53.7 us (22%)
  blocking collectives  26 us (11%)
  starting transfers between devices  24.2 us (10%)
  between operations  13.6 us (6%)
  other arithmetic  10.2 us (4%)
  local copies, waits for them, and re-layouts  4.46 us (2%)
    all_gather x1, waiting for transfers between devices, body(): weights = lax.all_gather(pieces, ('grp', 'dev'), axis=0, tiled=True)  78.8 us
    pallas_call x2, Pallas kernels, expert_half(): pl.pallas_call(expert_kernel, in_specs=[vmem, vmem, hbm, hbm], out_specs=...  34.1 us
    all_to_all x3, waiting for transfers between devices, shuffle(): lax.all_to_all(folded, 'dev', split_axis=0, concat_axis=0, tiled=True, ax...  26.6 us
    all_to_all x1, blocking collectives, shuffle(): lax.all_to_all(folded, 'dev', split_axis=0, concat_axis=0, tiled=True, ax...  26 us
    all_to_all x3, starting transfers between devices, shuffle(): lax.all_to_all(folded, 'dev', split_axis=0, concat_axis=0, tiled=True, ax...  23.6 us
    pallas_call x1, Pallas kernels, attention(): pl.pallas_call(attention_kernel, in_specs=[vmem] * 4 + [pl.BlockSpec(memo...  13.3 us
    pallas_call x1, Pallas kernels, combine(): pl.pallas_call(combine_kernel, in_specs=[pl.BlockSpec(memory_space=pltpu....  6.33 us
  transfers between devices with their start and end apart: 8, of which 5 were waited for; matrix products, arithmetic and copies ran while one was open for 3% of the time, Pallas kernels for 14%

profile of v2, /device:TPU:0, one launch (start us, length us, event | category | flops | bytes accessed | tf_op | source)
XLA Modules:
  0.0 243.6 jit_solution(4162883556085729223)
XLA Ops:
  6.5 1.6 pad_maximum_fusion
  8.1 0.6 broadcast.360
  8.7 1.5 reduce.3
  10.3 0.7 fusion.24
  11.2 1.4 convert_reduce_fusion
  13.3 0.7 slice_add_fusion
  14.5 78.8 %all-gather.2.cloned.1.call-done.weights = bf16[2048,4096]{1,0:T(8,128)(2,1)} async-done(((bf16[16,4096]{1,0:T(8,128)(2,1)}), bf16[2048,4096]{1,0:T(8,128)(2,1)}) %all-gather.2.cloned.1.call-update) | async-done | bytes 16777232 | tf_op jit(solution)/shard_map/all_gather | solution.py:278
  93.3 13.3 %attention.1 = (f32[256,2048]{1,0:T(8,128)}, bf16[512,1024]{1,0:T(8,128)(2,1)S(1)}, bf16[512,1536]{1,0:T(8,128)(2,1)}) custom-call(bf16[256,2048]{1,0:T(8,128)(2,1)S(1)} %fusion.5.xn, bf16[256,2048]{1,0:T(8,128)(2,1)S(1)} %copy-done, f32[6,2048]{1,0:T(8,128)S(1)} %reshape.273.mod, bf16[640,256]{1,0:T(8,128)(2,1)S(1)} %fusion.11.sel, ...), custom_call_target="tpu_custom_call" | custom-call | flops 7000000000 | bytes 24000000 | tf_op jit(solution)/shard_map/attention/pallas_call | solution.py:111
  106.6 26.0 %all_to_all.20 = bf16[64,8,1024]{2,1,0:T(8,128)(2,1)S(1)} all-to-all(bf16[64,8,1024]{2,1,0:T(8,128)(2,1)S(1)} %bitcast.25), channel_id=1, replica_groups={{0,21,42,63,4,25,46,51,8,29,34,55,12,17,38,59,1,22,43,60,5,26,47,48,9,3..., dimensions={0} | all-to-all | bytes 2097152 | tf_op jit(solution)/shard_map/all_to_all | solution.py:294
  132.6 6.3 %all-to-all-start = ((bf16[64,8,1536]{2,1,0:T(8,128)(2,1)}), bf16[64,8,1536]{2,1,0:T(8,128)(2,1)S(1)}, u32[]{:S(2)}, u32[]{:S(2)}) async-start(bf16[64,8,1536]{2,1,0:T(8,128)(2,1)} %bitcast.9), calls=%async_computation | async-start | bytes 3145728 | tf_op jit(solution)/shard_map/all_to_all | solution.py:294
  139.0 14.8 %experts.2 = (bf16[512,1024]{1,0:T(8,128)(2,1)S(1)}, bf16[512,1024]{1,0:T(8,128)(2,1)S(1)}) custom-call(bf16[512,1024]{1,0:T(8,128)(2,1)S(1)} %bitcast.24, bf16[512,1024]{1,0:T(8,128)(2,1)} %collective-permute-done.other, bf16[2048,2048]{1,0:T(8,128)(2,1)} %bitcast.38, bf16[2048,2048]{1,0:T(8,128)(2,1)} %bitcast.40), custom_call_target="tpu_custom_call" | custom-call | flops 8589934592 | bytes 25165824 | tf_op jit(solution)/shard_map/experts/pallas_call | solution.py:186
  154.1 2.4 collective-permute-done.1
  156.5 1.4 add_convert_fusion.1
  157.9 4.2 %all-to-all-done = bf16[64,8,1536]{2,1,0:T(8,128)(2,1)S(1)} async-done(((bf16[64,8,1536]{2,1,0:T(8,128)(2,1)}), bf16[64,8,1536]{2,1,0:T(8,128)(2,1)S(1)}, u32[]{:S(2)}, u32[]{:S(2)}) %all-to-all-start) | async-done | bytes 1572896 | tf_op jit(solution)/shard_map/all_to_all | solution.py:294
  162.1 6.9 %all-to-all-start.2 = ((bf16[64,8,1024]{2,1,0:T(8,128)(2,1)}), bf16[64,8,1024]{2,1,0:T(8,128)(2,1)}, u32[]{:S(2)}, u32[]{:S(2)}) async-start(bf16[64,8,1024]{2,1,0:T(8,128)(2,1)} %bitcast.26), calls=%async_computation.2 | async-start | bytes 2097152 | tf_op jit(solution)/shard_map/all_to_all | solution.py:294
  169.0 1.2 copy-done.2
  170.2 1.4 copy-done.3
  171.6 19.2 %experts.3 = (bf16[512,1536]{1,0:T(8,128)(2,1)S(1)}, bf16[512,1536]{1,0:T(8,128)(2,1)S(1)}) custom-call(bf16[512,1536]{1,0:T(8,128)(2,1)S(1)} %bitcast.21, bf16[512,1536]{1,0:T(8,128)(2,1)S(1)} %copy-done.3, bf16[2048,2048]{1,0:T(8,128)(2,1)} %bitcast.39, bf16[2048,2048]{1,0:T(8,128)(2,1)} %bitcast.41), custom_call_target="tpu_custom_call" | custom-call | flops 12884901888 | bytes 29360128 | tf_op jit(solution)/shard_map/experts/pallas_call | solution.py:186
  190.9 1.2 copy-done.1
  192.2 3.4 %collective-permute-done.3 = bf16[512,1536]{1,0:T(8,128)(2,1)S(1)} collective-permute-done((bf16[512,1536]{1,0:T(8,128)(2,1)}, bf16[512,1536]{1,0:T(8,128)(2,1)S(1)}, u32[]{:S(2)}, u32[]{:S(2)}) %collective-permute-start.3) | collective-permute-done | bytes 1572896 | tf_op jit(solution)/shard_map/ppermute | solution.py:309
  195.7 1.6 fusion.6
  197.2 10.5 %all-to-all-start.3 = ((bf16[64,8,1536]{2,1,0:T(8,128)(2,1)}), bf16[64,8,1536]{2,1,0:T(8,128)(2,1)S(1)}, u32[]{:S(2)}, u32[]{:S(2)}) async-start(bf16[64,8,1536]{2,1,0:T(8,128)(2,1)} %fusion.6), calls=%async_computation.3 | async-start | bytes 3145728 | tf_op jit(solution)/shard_map/all_to_all | solution.py:294
  208.1 22.4 %all-to-all-done.3 = bf16[64,8,1536]{2,1,0:T(8,128)(2,1)S(1)} async-done(((bf16[64,8,1536]{2,1,0:T(8,128)(2,1)}), bf16[64,8,1536]{2,1,0:T(8,128)(2,1)S(1)}, u32[]{:S(2)}, u32[]{:S(2)}) %all-to-all-start.3) | async-done | bytes 1572896 | tf_op jit(solution)/shard_map/all_to_all | solution.py:294
  230.4 6.3 %combine.1 = bf16[256,2048]{1,0:T(8,128)(2,1)} custom-call(f32[256,2048]{1,0:T(8,128)} %get-tuple-element.16.after_out, f32[6,2048]{1,0:T(8,128)S(1)} %reshape.273.mod, bf16[256,640]{1,0:T(8,128)(2,1)S(1)} %get-tuple-element.37.pick0, bf16[256,640]{1,0:T(8,128)(2,1)S(1)} %get-tuple-element.38.pick1, f32[256,2]{1,0:T(8,128)S(1)} %copy.11.prob, ...), custom_call_target="tpu_custom_call" | custom-call | flops 3000000000 | bytes 7000000 | tf_op jit(solution)/shard_map/combine/pallas_call | solution.py:231
  (30 shorter events, 2.2 us)
Async XLA Ops:
  6.5 6.1 %copy-start = (bf16[256,2048]{1,0:T(8,128)(2,1)S(1)}, bf16[256,2048]{1,0:T(8,128)(2,1)}, u32[]{:S(2)}) copy-start(bf16[256,2048]{1,0:T(8,128)(2,1)} %tok.1) | copy-start | bytes 3145732
  6.5 86.8 %all-gather.2.cloned.1.call-start = ((), (), s32[]{:S(2)}) async-start(), calls=%async_computation.4 | async-start | bytes 16908288 | tf_op jit(solution)/shard_map/all_gather | solution.py:278
  132.6 6.3 %collective-permute-start = (bf16[512,1024]{1,0:T(8,128)(2,1)S(1)}, bf16[512,1024]{1,0:T(8,128)(2,1)}, u32[]{:S(2)}, u32[]{:S(2)}) collective-permute-start(bf16[512,1024]{1,0:T(8,128)(2,1)S(1)} %bitcast.23), channel_id=1, source_target_pairs={{0,64},{64,0},{1,65},{65,1},{2,66},{66,2},{3,67},{67,3},{4,68},{68... | collective-permute-start | bytes 3145736 | tf_op jit(solution)/shard_map/ppermute | solution.py:302
  132.6 29.5 %all-to-all-start = ((bf16[64,8,1536]{2,1,0:T(8,128)(2,1)}), bf16[64,8,1536]{2,1,0:T(8,128)(2,1)S(1)}, u32[]{:S(2)}, u32[]{:S(2)}) async-start(bf16[64,8,1536]{2,1,0:T(8,128)(2,1)} %bitcast.9), calls=%async_computation | async-start | bytes 3145728 | tf_op jit(solution)/shard_map/all_to_all | solution.py:294
  153.8 2.7 %collective-permute-start.1 = (bf16[512,1024]{1,0:T(8,128)(2,1)S(1)}, bf16[512,1024]{1,0:T(8,128)(2,1)S(1)}, u32[]{:S(2)}, u32[]{:S(2)}) collective-permute-start(bf16[512,1024]{1,0:T(8,128)(2,1)S(1)} %get-tuple-element.20), channel_id=1, source_target_pairs={{0,64},{64,0},{1,65},{65,1},{2,66},{66,2},{3,67},{67,3},{4,68},{68... | collective-permute-start | bytes 3145736 | tf_op jit(solution)/shard_map/ppermute | solution.py:303
  162.1 6.9 %collective-permute-start.2 = (bf16[512,1536]{1,0:T(8,128)(2,1)S(1)}, bf16[512,1536]{1,0:T(8,128)(2,1)S(1)}, u32[]{:S(2)}, u32[]{:S(2)}) collective-permute-start(bf16[512,1536]{1,0:T(8,128)(2,1)S(1)} %bitcast.20), channel_id=1, source_target_pairs={{0,64},{64,0},{1,65},{65,1},{2,66},{66,2},{3,67},{67,3},{4,68},{68... | collective-permute-start | bytes 4718600 | tf_op jit(solution)/shard_map/ppermute | solution.py:306
  162.1 29.9 %all-to-all-start.2 = ((bf16[64,8,1024]{2,1,0:T(8,128)(2,1)}), bf16[64,8,1024]{2,1,0:T(8,128)(2,1)}, u32[]{:S(2)}, u32[]{:S(2)}) async-start(bf16[64,8,1024]{2,1,0:T(8,128)(2,1)} %bitcast.26), calls=%async_computation.2 | async-start | bytes 2097152 | tf_op jit(solution)/shard_map/all_to_all | solution.py:294
  169.0 1.2 copy-start.2
  170.2 1.4 copy-start.3
  190.9 1.2 copy-start.1
  192.0 3.6 %collective-permute-start.3 = (bf16[512,1536]{1,0:T(8,128)(2,1)}, bf16[512,1536]{1,0:T(8,128)(2,1)S(1)}, u32[]{:S(2)}, u32[]{:S(2)}) collective-permute-start(bf16[512,1536]{1,0:T(8,128)(2,1)} %copy-done.1), channel_id=1, source_target_pairs={{0,64},{64,0},{1,65},{65,1},{2,66},{66,2},{3,67},{67,3},{4,68},{68... | collective-permute-start | bytes 4718600 | tf_op jit(solution)/shard_map/ppermute | solution.py:309
  197.2 10.5 %copy-start.4 = (f32[256,2]{0,1:T(2,128)S(1)}, f32[256,2]{0,1:T(2,128)}, u32[]{:S(2)}) copy-start(f32[256,2]{0,1:T(2,128)} %param.19) | copy-start | bytes 6148
  197.2 33.2 %all-to-all-start.3 = ((bf16[64,8,1536]{2,1,0:T(8,128)(2,1)}), bf16[64,8,1536]{2,1,0:T(8,128)(2,1)S(1)}, u32[]{:S(2)}, u32[]{:S(2)}) async-start(bf16[64,8,1536]{2,1,0:T(8,128)(2,1)} %fusion.6), calls=%async_computation.3 | async-start | bytes 3145728 | tf_op jit(solution)/shard_map/all_to_all | solution.py:294
Sparse Core Ops, SparseCore 0:
  10.5 82.7 all-gather.1

commit v3 on v2

--- a/solution.py
+++ b/solution.py
@@ -9,7 +9,6 @@
 HDIM = 128
 TOP = 2
 CAP = 10
-PAIRS = (2, 3)
 TILE = 512
 WIDE = 1024
 TALL = 2048
@@ -46,8 +45,17 @@
     return mm(matrix, stacked).astype(BF16)
 
 
-def attention_kernel(xn, tok, mod, sel, weights, after_out, *rest):
-    sends, (after, mixed, held, sems) = rest[: len(PAIRS)], rest[len(PAIRS) :]
+def unfold_into(target, top, folded):
+    matrix = fold_matrix(True)
+    for g in range(2):
+        flat = mm(matrix, folded[g * 256 : (g + 1) * 256, :]).astype(BF16)
+        for q in range(4):
+            target[top + g * 64 : top + (g + 1) * 64, q * 512 : (q + 1) * 512] = flat[
+                q * 64 : (q + 1) * 64, :
+            ]
+
+
+def attention_kernel(xn, tok, mod, sel, weights, after_out, send, after, mixed, held, sems):
     width, inner = xn.shape[1], mixed.shape[1]
     groups = inner // WIDE
     copies = []
@@ -91,16 +99,12 @@
     keep = pltpu.make_async_copy(after, after_out, sems.at[len(copies)])
     keep.start()
     normed = (normalize(after[...]) * (1.0 + mod[4:5, :]) + mod[3:4, :]).astype(BF16)
+    whole = sel.shape[0] * 4 // 5
+    send[:, :width] = mm(sel[:whole, :], normed).astype(BF16)
+    rows = mm(sel[whole:, :], normed).astype(BF16)
     matrix = fold_matrix(False)
-    pair = 0
-    for send in sends:
-        for j in range(send.shape[1] // 512):
-            rows = mm(sel[pair * 128 : (pair + 1) * 128, :], normed).astype(BF16)
-            for g in range(2):
-                send[g * 256 : (g + 1) * 256, j * 512 : (j + 1) * 512] = fold(
-                    rows[g * 64 : (g + 1) * 64, :], matrix
-                )
-            pair += 1
+    for g in range(2):
+        send[g * 256 : (g + 1) * 256, width:] = fold(rows[g * 64 : (g + 1) * 64, :], matrix)
     keep.wait()
 
 
@@ -111,9 +115,11 @@
     return pl.pallas_call(
         attention_kernel,
         in_specs=[vmem] * 4 + [pl.BlockSpec(memory_space=pltpu.HBM)],
-        out_specs=[pl.BlockSpec(memory_space=pltpu.HBM)] + [vmem] * len(PAIRS),
-        out_shape=[pltpu.HBM((rows, width), F32)]
-        + [jax.ShapeDtypeStruct((512, 512 * n), BF16) for n in PAIRS],
+        out_specs=[pl.BlockSpec(memory_space=pltpu.HBM), vmem],
+        out_shape=[
+            pltpu.HBM((rows, width), F32),
+            jax.ShapeDtypeStruct((sel.shape[0] * 4 // 5, width * 5 // 4), BF16),
+        ],
         scratch_shapes=[
             pltpu.VMEM((rows, width), F32),
             pltpu.VMEM((rows, inner), BF16),
@@ -128,10 +134,10 @@
     )(xn, tok, mod, sel, in_hbm(weights))
 
 
-def expert_kernel(own, other, w_first, w_second, own_out, other_out, x, hidden, first, second, sems):
-    pairs = own.shape[1] // 512
-    tiles = first.shape[1] // TILE
-    blocks = [(src, j) for src in range(2) for j in range(pairs)]
+def expert_kernel(own, other, w_first, w_second, own_out, other_out, last, hidden, first, second, sems):
+    width, half = first.shape
+    tiles = half // TILE
+    whole = own.shape[0]
 
     def fetch(which, n):
         source, target = ((w_first, first), (w_second, second))[which]
@@ -144,43 +150,40 @@
         for n in range(tiles):
             fetch(which, n).start()
 
-    matrix = fold_matrix(True)
-    for n, (src, j) in enumerate(blocks):
-        ref = (own, other)[src]
-        for g in range(2):
-            flat = mm(matrix, ref[g * 256 : (g + 1) * 256, j * 512 : (j + 1) * 512]).astype(BF16)
-            for q in range(4):
-                x[n * 128 + g * 64 : n * 128 + (g + 1) * 64, q * 512 : (q + 1) * 512] = flat[
-                    q * 64 : (q + 1) * 64, :
-                ]
+    unfold_into(last, 0, own[:, width:])
+    unfold_into(last, whole // 4, other[:, width:])
 
     @pl.loop(0, tiles)
     def _(n):
         fetch(0, n).wait()
         cut = pl.ds(pl.multiple_of(n * TILE, TILE), TILE)
-        for m in range(0, x.shape[0], MB):
-            product = mm(x[m : m + MB, :], first[:, cut])
-            hidden[m : m + MB, cut] = jax.nn.gelu(product, approximate=True).astype(BF16)
+        for at, rows in enumerate((own, other, last)):
+            for m in range(0, rows.shape[0], MB):
+                product = mm(rows[m : m + MB, :width], first[:, cut])
+                hidden[at * whole + m : at * whole + m + MB, cut] = jax.nn.gelu(
+                    product, approximate=True
+                ).astype(BF16)
 
     @pl.loop(0, tiles)
     def _(n):
         fetch(1, n).wait()
         cut = pl.ds(pl.multiple_of(n * TILE, TILE), TILE)
-        for m in range(0, x.shape[0], MB):
-            x[m : m + MB, cut] = mm(hidden[m : m + MB, :], second[:, cut]).astype(BF16)
+        for at, rows in enumerate((own_out, other_out, last)):
+            for m in range(0, rows.shape[0], MB):
+                rows[m : m + MB, cut] = mm(
+                    hidden[at * whole + m : at * whole + m + MB, :], second[:, cut]
+                ).astype(BF16)
 
     matrix = fold_matrix(False)
-    for n, (src, j) in enumerate(blocks):
-        ref = (own_out, other_out)[src]
+    for at, rows in enumerate((own_out, other_out)):
         for g in range(2):
-            ref[g * 256 : (g + 1) * 256, j * 512 : (j + 1) * 512] = fold(
-                x[n * 128 + g * 64 : n * 128 + (g + 1) * 64, :], matrix
-            )
+            top = at * (whole // 4) + g * 64
+            rows[g * 256 : (g + 1) * 256, width:] = fold(last[top : top + 64, :], matrix)
 
 
 def expert_half(own, other, w_first, w_second):
     width, half = w_first.shape
-    rows = own.shape[1] // 2
+    rows = own.shape[0] * 5 // 2
     vmem = pl.BlockSpec(memory_space=pltpu.VMEM)
     hbm = pl.BlockSpec(memory_space=pltpu.HBM)
     return pl.pallas_call(
@@ -189,13 +192,13 @@
         out_specs=[vmem, vmem],
         out_shape=[jax.ShapeDtypeStruct(own.shape, BF16)] * 2,
         scratch_shapes=[
-            pltpu.VMEM((rows, width), BF16),
+            pltpu.VMEM((own.shape[0] // 2, width), BF16),
             pltpu.VMEM((rows, half), BF16),
             pltpu.VMEM((width, half), BF16),
             pltpu.VMEM((half, width), BF16),
             pltpu.SemaphoreType.DMA((2 * (half // TILE),)),
         ],
-        compiler_params=pltpu.CompilerParams(vmem_limit_bytes=25 * MIB),
+        compiler_params=pltpu.CompilerParams(vmem_limit_bytes=28 * MIB),
         cost_estimate=pl.CostEstimate(
             flops=4 * rows * width * half,
             transcendentals=rows * half,
@@ -205,45 +208,51 @@
     )(own, other, in_hbm(w_first), in_hbm(w_second))
 
 
-def combine_kernel(after_out, mod, pick0, pick1, prob, *rest):
-    backs, (result, after, flat, sem) = rest[: len(PAIRS)], rest[len(PAIRS) :]
+def combine_kernel(after_out, mod, pick0, pick1, prob, back, result_out, after, last, result, sem, sems):
     kept = pltpu.make_async_copy(after_out, after, sem)
     kept.start()
-    matrix = fold_matrix(True)
-    top = 0
-    for back in backs:
-        for j in range(back.shape[1] // 512):
-            for g in range(2):
-                rows = mm(matrix, back[g * 256 : (g + 1) * 256, j * 512 : (j + 1) * 512]).astype(BF16)
-                for q in range(4):
-                    flat[top : top + 64, q * 512 : (q + 1) * 512] = rows[q * 64 : (q + 1) * 64, :]
-                top += 64
-    kept.wait()
+    rows, width = after.shape
+    whole = back.shape[0]
+    unfold_into(last, 0, back[:, width:])
+    copies = []
     for q in range(4):
         cut = slice(q * 512, (q + 1) * 512)
-        mix = prob[:, 0:1] * mm(pick0[...], flat[:, cut]) + prob[:, 1:2] * mm(pick1[...], flat[:, cut])
+        picked = [
+            mm(pick[:, :whole], back[:, cut]) + mm(pick[:, whole:], last[:, cut])
+            for pick in (pick0, pick1)
+        ]
+        mix = prob[:, 0:1] * picked[0] + prob[:, 1:2] * picked[1]
+        if q == 0:
+            kept.wait()
         result[:, cut] = (after[:, cut] + mod[5:6, cut] * mix).astype(BF16)
-
-
-def combine(after, mod, pick0, pick1, prob, backs):
+        copies.append(pltpu.make_async_copy(result.at[:, cut], result_out.at[:, cut], sems.at[q]))
+        copies[-1].start()
+    for copy in copies:
+        copy.wait()
+
+
+def combine(after, mod, pick0, pick1, prob, back):
     rows, width = after.shape
     vmem = pl.BlockSpec(memory_space=pltpu.VMEM)
+    hbm = pl.BlockSpec(memory_space=pltpu.HBM)
     return pl.pallas_call(
         combine_kernel,
-        in_specs=[pl.BlockSpec(memory_space=pltpu.HBM)] + [vmem] * (4 + len(backs)),
-        out_specs=vmem,
+        in_specs=[hbm] + [vmem] * 5,
+        out_specs=hbm,
         out_shape=jax.ShapeDtypeStruct((rows, width), BF16),
         scratch_shapes=[
             pltpu.VMEM((rows, width), F32),
-            pltpu.VMEM((128 * sum(PAIRS), width), BF16),
+            pltpu.VMEM((back.shape[0] // 4, width), BF16),
+            pltpu.VMEM((rows, width), BF16),
             pltpu.SemaphoreType.DMA,
+            pltpu.SemaphoreType.DMA((4,)),
         ],
         compiler_params=pltpu.CompilerParams(vmem_limit_bytes=16 * MIB),
         cost_estimate=pl.CostEstimate(
             flops=3 * 10**9, transcendentals=0, bytes_accessed=7 * 10**6
         ),
         name="combine",
-    )(in_hbm(after), mod, pick0, pick1, prob, *backs)
+    )(in_hbm(after), mod, pick0, pick1, prob, back)
 
 
 def diagonal_order(experts):
@@ -267,7 +276,8 @@
     slots = []
     for k in range(TOP):
         rank = jnp.sum(jnp.where(chosen[k], before, 0.0), axis=1).astype(jnp.int32)
-        slots.append((rank // 2) * (2 * experts) + routes[:, k] * 2 + rank % 2)
+        place = routes[:, k]
+        slots.append(jnp.where(rank < 8, place * 8 + rank, 8 * experts + place * 2 + rank - 8))
     return slots
 
 
@@ -285,7 +295,7 @@
     sel = sum((ids[:, None] == s[None, :]).astype(BF16) for s in slots)
     picks = [(s[:, None] == ids[None, :]).astype(BF16) for s in slots]
 
-    after, *sends = attention(xn, tokens, mod, sel, weights)
+    after, send = attention(xn, tokens, mod, sel, weights)
     swap = [(0, 1), (1, 0)]
 
     def shuffle(rows):
@@ -298,17 +308,10 @@
     add = lambda a, b: (a.astype(F32) + b.astype(F32)).astype(BF16)
     w_first, w_second = w_in[0], w_back[0]
 
-    own_a, own_b = [shuffle(send) for send in sends]
-    mine_a, theirs_a = expert_half(own_a, lax.ppermute(own_a, "grp", swap), w_first, w_second)
-    total_a = add(mine_a, lax.ppermute(theirs_a, "grp", swap))
-    own_b, total_a = lax.optimization_barrier((own_b, total_a))
-    back_a = shuffle(total_a)
-    other_b = lax.ppermute(own_b, "grp", swap)
-    mine_b, theirs_b = expert_half(own_b, other_b, w_first, w_second)
-    back_a, theirs_b = lax.optimization_barrier((back_a, theirs_b))
-    total_b = add(mine_b, lax.ppermute(theirs_b, "grp", swap))
-    backs = [back_a, shuffle(total_b)]
-    return combine(after, mod, picks[0], picks[1], route_prob, backs)
+    own = shuffle(send)
+    mine, theirs = expert_half(own, lax.ppermute(own, "grp", swap), w_first, w_second)
+    back = shuffle(add(mine, lax.ppermute(theirs, "grp", swap)))
+    return combine(after, mod, picks[0], picks[1], route_prob, back)
 
 
 def solution(mesh):

time: 244 us -> 238 us (0.975)
  starting transfers between devices: 24.2 us -> 6.17 us
  blocking collectives: 26 us -> 43.4 us
  Pallas kernels: 53.7 us -> 41.4 us
  waiting for transfers between devices: 111 us -> 122 us
  local copies, waits for them, and re-layouts: 4.46 us -> 0.7 us
    all_to_all x3 -> x1, starting transfers between devices: 23.6 us -> 5.94 us  [shuffle(): lax.all_to_all(folded, 'dev', split_axis=0, concat_axis=0, tiled=True, ax...]
    all_to_all x1, blocking collectives: 26 us -> 43.4 us  [shuffle(): lax.all_to_all(folded, 'dev', split_axis=0, concat_axis=0, tiled=True, ax...]
    all_to_all x3 -> x1, waiting for transfers between devices: 26.6 us -> 33.7 us  [shuffle(): lax.all_to_all(folded, 'dev', split_axis=0, concat_axis=0, tiled=True, ax...]
    pallas_call x2 -> x1, Pallas kernels: 34.1 us -> 27.5 us  [expert_half(): pl.pallas_call(expert_kernel, in_specs=[vmem, vmem, hbm, hbm], out_specs=...]
    ppermute x4 -> x2, waiting for transfers between devices: 5.85 us -> 9.68 us  [the longest x1 4.91 us: body(): lax.ppermute(own, 'grp', swap)]
    unnamed x12 -> x6, local copies, waits for them, and re-layouts: 4.45 us -> 0.68 us
    pallas_call x1, Pallas kernels: 13.3 us -> 10 us  [attention(): pl.pallas_call(attention_kernel, in_specs=[vmem] * 4 + [pl.BlockSpec(memo...]
    pallas_call x1, Pallas kernels: 6.33 us -> 3.83 us  [combine(): pl.pallas_call(combine_kernel, in_specs=[hbm] + [vmem] * 5, out_specs=hbm...]
  transfers between devices with their start and end apart: 8 -> 4, of which waited for: 5 -> 4; matrix products, arithmetic and copies ran while one was open for 3% -> 3% of each run, Pallas kernels for 14% -> 0%
where the time goes in v3:
time: 238 us; the launch traced here: 237 us
  waiting for transfers between devices  122 us (51%)
  blocking collectives  43.4 us (18%)
  Pallas kernels  41.4 us (17%)
  between operations  13.5 us (6%)
  other arithmetic  9.42 us (4%)
  starting transfers between devices  6.17 us (3%)
    all_gather x1, waiting for transfers between devices, body(): weights = lax.all_gather(pieces, ('grp', 'dev'), axis=0, tiled=True)  78.9 us
    all_to_all x1, blocking collectives, shuffle(): lax.all_to_all(folded, 'dev', split_axis=0, concat_axis=0, tiled=True, ax...  43.4 us
    all_to_all x1, waiting for transfers between devices, shuffle(): lax.all_to_all(folded, 'dev', split_axis=0, concat_axis=0, tiled=True, ax...  33.7 us
    pallas_call x1, Pallas kernels, expert_half(): pl.pallas_call(expert_kernel, in_specs=[vmem, vmem, hbm, hbm], out_specs=...  27.5 us
    pallas_call x1, Pallas kernels, attention(): pl.pallas_call(attention_kernel, in_specs=[vmem] * 4 + [pl.BlockSpec(memo...  10 us
    all_to_all x1, starting transfers between devices, shuffle(): lax.all_to_all(folded, 'dev', split_axis=0, concat_axis=0, tiled=True, ax...  5.94 us
    ppermute x1, waiting for transfers between devices, body(): lax.ppermute(own, 'grp', swap)  4.91 us
    ppermute x1, waiting for transfers between devices, body(): back = shuffle(add(mine, lax.ppermute(theirs, 'grp', swap)))  4.77 us
  transfers between devices with their start and end apart: 4, of which 4 were waited for; matrix products, arithmetic and copies ran while one was open for 3% of the time, Pallas kernels for 0%

profile of v3, /device:TPU:0, one launch (start us, length us, event | category | flops | bytes accessed | tf_op | source)
XLA Modules:
  0.0 237.0 jit_solution(8414570804164246337)
XLA Ops:
  6.5 1.6 pad_maximum_fusion
  8.1 0.0 all-gather.2.cloned.1.call-update
  8.1 0.5 broadcast.162
  8.7 1.5 reduce.3
  10.2 0.7 fusion.24
  11.0 0.2 select_reduce_fusion.1
  11.2 1.4 convert_reduce_fusion
  12.6 0.4 fusion.3
  13.1 0.2 fusion.11.sel
  13.3 0.7 slice_add_fusion
  14.0 0.5 fusion.6.xn
  14.5 78.9 %all-gather.2.cloned.1.call-done.weights = bf16[2048,4096]{1,0:T(8,128)(2,1)} async-done(((bf16[16,4096]{1,0:T(8,128)(2,1)}), bf16[2048,4096]{1,0:T(8,128)(2,1)}) %all-gather.2.cloned.1.call-update) | async-done | bytes 16777232 | tf_op jit(solution)/shard_map/all_gather | solution.py:288
  93.3 10.0 %attention.1 = (f32[256,2048]{1,0:T(8,128)}, bf16[512,2560]{1,0:T(8,128)(2,1)S(1)}) custom-call(bf16[256,2048]{1,0:T(8,128)(2,1)S(1)} %fusion.6.xn, bf16[256,2048]{1,0:T(8,128)(2,1)S(1)} %copy-done, f32[6,2048]{1,0:T(8,128)S(1)} %reshape.95.mod, bf16[640,256]{1,0:T(8,128)(2,1)S(1)} %fusion.11.sel, bf16[2048,4096]{1,0:T(8,128)(2,1)} %all-gather.2.cloned.1.call-done.weights), custom_call_target="tpu_custom_call" | custom-call | flops 7000000000 | bytes 24000000 | tf_op jit(solution)/shard_map/attention/pallas_call | solution.py:115
  103.4 43.4 %all_to_all.10 = bf16[64,8,2560]{2,1,0:T(8,128)(2,1)S(1)} all-to-all(bf16[64,8,2560]{2,1,0:T(8,128)(2,1)S(1)} %bitcast.19), channel_id=1, replica_groups={{0,21,42,63,4,25,46,51,8,29,34,55,12,17,38,59,1,22,43,60,5,26,47,48,9,3..., dimensions={0} | all-to-all | bytes 5242880 | tf_op jit(solution)/shard_map/all_to_all | solution.py:304
  146.8 4.9 %collective-permute-done.other = bf16[512,2560]{1,0:T(8,128)(2,1)S(1)} collective-permute-done((bf16[512,2560]{1,0:T(8,128)(2,1)S(1)}, bf16[512,2560]{1,0:T(8,128)(2,1)S(1)}, u32[]{:S(2)}, u32[]{:S(2)}) %collective-permute-start) | collective-permute-done | bytes 2621472 | tf_op jit(solution)/shard_map/ppermute | solution.py:312
  151.7 27.5 %experts.1 = (bf16[512,2560]{1,0:T(8,128)(2,1)S(1)}, bf16[512,2560]{1,0:T(8,128)(2,1)S(1)}) custom-call(bf16[512,2560]{1,0:T(8,128)(2,1)S(1)} %bitcast.18, bf16[512,2560]{1,0:T(8,128)(2,1)S(1)} %collective-permute-done.other, bf16[2048,2048]{1,0:T(8,128)(2,1)} %bitcast.31, bf16[2048,2048]{1,0:T(8,128)(2,1)} %bitcast.32), custom_call_target="tpu_custom_call" | custom-call | flops 21474836480 | bytes 37748736 | tf_op jit(solution)/shard_map/experts/pallas_call | solution.py:189
  179.2 0.2 collective-permute-start.1
  179.5 4.8 %collective-permute-done.1 = bf16[512,2560]{1,0:T(8,128)(2,1)S(1)} collective-permute-done((bf16[512,2560]{1,0:T(8,128)(2,1)S(1)}, bf16[512,2560]{1,0:T(8,128)(2,1)S(1)}, u32[]{:S(2)}, u32[]{:S(2)}) %collective-permute-start.1) | collective-permute-done | bytes 2621472 | tf_op jit(solution)/shard_map/ppermute | solution.py:313
  184.2 2.1 fusion
  186.4 5.9 %all-to-all-start.1 = ((bf16[64,8,2560]{2,1,0:T(8,128)(2,1)}), bf16[64,8,2560]{2,1,0:T(8,128)(2,1)S(1)}, u32[]{:S(2)}, u32[]{:S(2)}) async-start(bf16[64,8,2560]{2,1,0:T(8,128)(2,1)} %fusion), calls=%async_computation.1 | async-start | bytes 5242880 | tf_op jit(solution)/shard_map/all_to_all | solution.py:304
  192.4 0.1 copy.11.prob
  192.5 0.2 fusion.9
  192.7 33.7 %all-to-all-done.1 = bf16[64,8,2560]{2,1,0:T(8,128)(2,1)S(1)} async-done(((bf16[64,8,2560]{2,1,0:T(8,128)(2,1)}), bf16[64,8,2560]{2,1,0:T(8,128)(2,1)S(1)}, u32[]{:S(2)}, u32[]{:S(2)}) %all-to-all-start.1) | async-done | bytes 2621472 | tf_op jit(solution)/shard_map/all_to_all | solution.py:304
  226.4 3.8 %combine.1 = bf16[256,2048]{1,0:T(8,128)(2,1)} custom-call(f32[256,2048]{1,0:T(8,128)} %get-tuple-element.9.after_out, f32[6,2048]{1,0:T(8,128)S(1)} %reshape.95.mod, bf16[256,640]{1,0:T(8,128)(2,1)S(1)} %get-tuple-element.23.pick0, bf16[256,640]{1,0:T(8,128)(2,1)S(1)} %get-tuple-element.24.pick1, f32[256,2]{1,0:T(8,128)S(1)} %copy.11.prob, ...), custom_call_target="tpu_custom_call" | custom-call | flops 3000000000 | bytes 7000000 | tf_op jit(solution)/shard_map/combine/pallas_call | solution.py:238
  (14 shorter events, 0.1 us)
Async XLA Ops:
  6.5 6.1 %copy-start = (bf16[256,2048]{1,0:T(8,128)(2,1)S(1)}, bf16[256,2048]{1,0:T(8,128)(2,1)}, u32[]{:S(2)}) copy-start(bf16[256,2048]{1,0:T(8,128)(2,1)} %tok.1) | copy-start | bytes 3145732
  6.5 86.8 %all-gather.2.cloned.1.call-start = ((), (), s32[]{:S(2)}) async-start(), calls=%async_computation.2 | async-start | bytes 16908288 | tf_op jit(solution)/shard_map/all_gather | solution.py:288
  146.8 4.9 %collective-permute-start = (bf16[512,2560]{1,0:T(8,128)(2,1)S(1)}, bf16[512,2560]{1,0:T(8,128)(2,1)S(1)}, u32[]{:S(2)}, u32[]{:S(2)}) collective-permute-start(bf16[512,2560]{1,0:T(8,128)(2,1)S(1)} %bitcast.17), channel_id=1, source_target_pairs={{0,64},{64,0},{1,65},{65,1},{2,66},{66,2},{3,67},{67,3},{4,68},{68... | collective-permute-start | bytes 7864328 | tf_op jit(solution)/shard_map/ppermute | solution.py:312
  179.2 5.0 %collective-permute-start.1 = (bf16[512,2560]{1,0:T(8,128)(2,1)S(1)}, bf16[512,2560]{1,0:T(8,128)(2,1)S(1)}, u32[]{:S(2)}, u32[]{:S(2)}) collective-permute-start(bf16[512,2560]{1,0:T(8,128)(2,1)S(1)} %get-tuple-element.12), channel_id=1, source_target_pairs={{0,64},{64,0},{1,65},{65,1},{2,66},{66,2},{3,67},{67,3},{4,68},{68... | collective-permute-start | bytes 7864328 | tf_op jit(solution)/shard_map/ppermute | solution.py:313
  186.4 6.0 %copy-start.1 = (f32[256,2]{0,1:T(2,128)S(1)}, f32[256,2]{0,1:T(2,128)}, u32[]{:S(2)}) copy-start(f32[256,2]{0,1:T(2,128)} %param.19) | copy-start | bytes 6148
  186.4 40.0 %all-to-all-start.1 = ((bf16[64,8,2560]{2,1,0:T(8,128)(2,1)}), bf16[64,8,2560]{2,1,0:T(8,128)(2,1)S(1)}, u32[]{:S(2)}, u32[]{:S(2)}) async-start(bf16[64,8,2560]{2,1,0:T(8,128)(2,1)} %fusion), calls=%async_computation.1 | async-start | bytes 5242880 | tf_op jit(solution)/shard_map/all_to_all | solution.py:304
Sparse Core Ops, SparseCore 0:
  10.5 82.7 all-gather.1

commit v4 on v3

--- a/solution.py
+++ b/solution.py
@@ -1,3 +1,5 @@
+import functools
+
 import jax
 import jax.numpy as jnp
 from jax import lax
@@ -11,8 +13,7 @@
 CAP = 10
 TILE = 512
 WIDE = 1024
-TALL = 2048
-MB = 256
+MB = 640
 BF16 = jnp.bfloat16
 F32 = jnp.float32
 MIB = 1024 * 1024
@@ -58,26 +59,38 @@
 def attention_kernel(xn, tok, mod, sel, weights, after_out, send, after, mixed, held, sems):
     width, inner = xn.shape[1], mixed.shape[1]
     groups = inner // WIDE
+    cores = weights.shape[1]
     copies = []
 
-    def fetch(rows, cols):
+    def fetch(first, count):
+        cut = pl.ds(first, count)
         copies.append(
-            pltpu.make_async_copy(weights.at[rows, cols], held.at[rows, cols], sems.at[len(copies)])
+            [
+                pltpu.make_async_copy(
+                    weights.at[:, core, :, cut], held.at[core, :, :, cut], sems.at[len(copies), core]
+                )
+                for core in range(cores)
+            ]
         )
-        copies[-1].start()
+        for copy in copies[-1]:
+            copy.start()
+
+    def arrived(n, cut):
+        for copy in copies[n]:
+            copy.wait()
+        return held[:, :, :, cut].reshape(width, cut.stop - cut.start)
 
     for n in range(groups):
         for part in range(3):
-            fetch(pl.ds(0, width), pl.ds(part * inner + n * WIDE, WIDE))
-    for n in range(width // TALL):
-        fetch(pl.ds(n * TALL, TALL), pl.ds(3 * inner, inner))
+            fetch(part * inner + n * WIDE, WIDE)
+    fetch(3 * inner, inner)
 
     for n in range(groups):
         projections = []
         for part in range(3):
-            copies[3 * n + part].wait()
             first = part * inner + n * WIDE
-            projections.append(mm(xn[...], held[:, first : first + WIDE]).astype(BF16))
+            block = arrived(3 * n + part, slice(first, first + WIDE))
+            projections.append(mm(xn[...], block).astype(BF16))
         q, k, v = projections
         for h in range(WIDE // HDIM):
             cut = slice(h * HDIM, (h + 1) * HDIM)
@@ -88,15 +101,15 @@
             attn = (exponent / jnp.sum(exponent, axis=-1, keepdims=True)).astype(BF16)
             mixed[:, n * WIDE + h * HDIM : n * WIDE + (h + 1) * HDIM] = mm(attn, v[:, cut]).astype(BF16)
 
-    for n in range(width // TALL):
-        copies[3 * groups + n].wait()
-        cut = slice(n * TALL, (n + 1) * TALL)
-        projected = lax.dot_general(
-            mixed[...], held[cut, 3 * inner :], (((1,), (1,)), ((), ())), preferred_element_type=F32
-        )
-        after[:, cut] = tok[:, cut].astype(F32) + mod[2:3, cut] * projected
-
-    keep = pltpu.make_async_copy(after, after_out, sems.at[len(copies)])
+    projected = lax.dot_general(
+        mixed[...],
+        arrived(3 * groups, slice(3 * inner, 4 * inner)),
+        (((1,), (1,)), ((), ())),
+        preferred_element_type=F32,
+    )
+    after[...] = tok[...].astype(F32) + mod[2:3, :] * projected
+
+    keep = pltpu.make_async_copy(after, after_out, sems.at[len(copies), 0])
     keep.start()
     normed = (normalize(after[...]) * (1.0 + mod[4:5, :]) + mod[3:4, :]).astype(BF16)
     whole = sel.shape[0] * 4 // 5
@@ -123,8 +136,8 @@
         scratch_shapes=[
             pltpu.VMEM((rows, width), F32),
             pltpu.VMEM((rows, inner), BF16),
-            pltpu.VMEM((width, 4 * inner), BF16),
-            pltpu.SemaphoreType.DMA((3 * (inner // WIDE) + width // TALL + 1,)),
+            pltpu.VMEM((weights.shape[1], weights.shape[0], *weights.shape[2:]), BF16),
+            pltpu.SemaphoreType.DMA((3 * (inner // WIDE) + 2, weights.shape[1])),
         ],
         compiler_params=pltpu.CompilerParams(vmem_limit_bytes=26 * MIB),
         cost_estimate=pl.CostEstimate(
@@ -134,78 +147,87 @@
     )(xn, tok, mod, sel, in_hbm(weights))
 
 
-def expert_kernel(own, other, w_first, w_second, own_out, other_out, last, hidden, first, second, sems):
-    width, half = first.shape
-    tiles = half // TILE
-    whole = own.shape[0]
+def experts_kernel(has_first, has_second, *refs):
+    refs = list(refs)
+    source = refs.pop(0)
+    weights = [refs.pop(0) for _ in range(has_first + has_second)]
+    out = refs.pop(0)
+    held = [refs.pop(0) for _ in weights]
+    x, hidden, sems = refs
+    width = x.shape[1]
+    whole = x.shape[0] * 4 // 5
+    tiles = width // TILE
 
     def fetch(which, n):
-        source, target = ((w_first, first), (w_second, second))[which]
         cut = pl.ds(pl.multiple_of(n * TILE, TILE), TILE)
         return pltpu.make_async_copy(
-            source.at[:, cut], target.at[:, cut], sems.at[which * tiles + n]
+            weights[which].at[:, cut], held[which].at[:, cut], sems.at[which, n]
         )
 
-    for which in range(2):
+    for which in range(len(weights)):
         for n in range(tiles):
             fetch(which, n).start()
 
-    unfold_into(last, 0, own[:, width:])
-    unfold_into(last, whole // 4, other[:, width:])
-
-    @pl.loop(0, tiles)
-    def _(n):
-        fetch(0, n).wait()
-        cut = pl.ds(pl.multiple_of(n * TILE, TILE), TILE)
-        for at, rows in enumerate((own, other, last)):
-            for m in range(0, rows.shape[0], MB):
-                product = mm(rows[m : m + MB, :width], first[:, cut])
-                hidden[at * whole + m : at * whole + m + MB, cut] = jax.nn.gelu(
-                    product, approximate=True
-                ).astype(BF16)
-
-    @pl.loop(0, tiles)
-    def _(n):
-        fetch(1, n).wait()
-        cut = pl.ds(pl.multiple_of(n * TILE, TILE), TILE)
-        for at, rows in enumerate((own_out, other_out, last)):
-            for m in range(0, rows.shape[0], MB):
-                rows[m : m + MB, cut] = mm(
-                    hidden[at * whole + m : at * whole + m + MB, :], second[:, cut]
-                ).astype(BF16)
-
-    matrix = fold_matrix(False)
-    for at, rows in enumerate((own_out, other_out)):
+    if has_first:
+        x[:whole, :] = source[:, :width]
+        unfold_into(x, whole, source[:, width:])
+        target = hidden if has_second else out
+
+        @pl.loop(0, tiles)
+        def _(n):
+            fetch(0, n).wait()
+            cut = pl.ds(pl.multiple_of(n * TILE, TILE), TILE)
+            for m in range(0, x.shape[0], MB):
+                product = mm(x[m : m + MB, :], held[0][:, cut])
+                target[m : m + MB, cut] = jax.nn.gelu(product, approximate=True).astype(BF16)
+
+    if has_second:
+        inner = hidden if has_first else source
+
+        @pl.loop(0, tiles)
+        def _(n):
+            fetch(len(weights) - 1, n).wait()
+            cut = pl.ds(pl.multiple_of(n * TILE, TILE), TILE)
+            for m in range(0, x.shape[0], MB):
+                product = mm(inner[m : m + MB, :], held[-1][:, cut]).astype(BF16)
+                direct = min(max(whole - m, 0), MB)
+                if direct:
+                    out[m : m + direct, cut] = product[:direct]
+                if direct < MB:
+                    x[m + direct : m + MB, cut] = product[direct:]
+
+        matrix = fold_matrix(False)
         for g in range(2):
-            top = at * (whole // 4) + g * 64
-            rows[g * 256 : (g + 1) * 256, width:] = fold(last[top : top + 64, :], matrix)
-
-
-def expert_half(own, other, w_first, w_second):
-    width, half = w_first.shape
-    rows = own.shape[0] * 5 // 2
+            top = whole + g * 64
+            out[g * 256 : (g + 1) * 256, width:] = fold(x[top : top + 64, :], matrix)
+
+
+def expert_rows(source, rows, w_first=None, w_second=None):
+    weights = [in_hbm(w) for w in (w_first, w_second) if w is not None]
+    has_first, has_second = w_first is not None, w_second is not None
+    half, width = weights[0].shape
     vmem = pl.BlockSpec(memory_space=pltpu.VMEM)
     hbm = pl.BlockSpec(memory_space=pltpu.HBM)
+    shape = (rows * 4 // 5, width * 5 // 4) if has_second else (rows, half)
     return pl.pallas_call(
-        expert_kernel,
-        in_specs=[vmem, vmem, hbm, hbm],
-        out_specs=[vmem, vmem],
-        out_shape=[jax.ShapeDtypeStruct(own.shape, BF16)] * 2,
-        scratch_shapes=[
-            pltpu.VMEM((own.shape[0] // 2, width), BF16),
-            pltpu.VMEM((rows, half), BF16),
-            pltpu.VMEM((width, half), BF16),
-            pltpu.VMEM((half, width), BF16),
-            pltpu.SemaphoreType.DMA((2 * (half // TILE),)),
+        functools.partial(experts_kernel, has_first, has_second),
+        in_specs=[vmem] + [hbm] * len(weights),
+        out_specs=vmem,
+        out_shape=jax.ShapeDtypeStruct(shape, BF16),
+        scratch_shapes=[pltpu.VMEM(w.shape, BF16) for w in weights]
+        + [
+            pltpu.VMEM((rows, width), BF16),
+            pltpu.VMEM((rows, half) if has_first and has_second else (8, 128), BF16),
+            pltpu.SemaphoreType.DMA((len(weights), width // TILE)),
         ],
-        compiler_params=pltpu.CompilerParams(vmem_limit_bytes=28 * MIB),
+        compiler_params=pltpu.CompilerParams(vmem_limit_bytes=(10 + 9 * len(weights)) * MIB),
         cost_estimate=pl.CostEstimate(
-            flops=4 * rows * width * half,
-            transcendentals=rows * half,
-            bytes_accessed=4 * width * half + 8 * rows * width,
+            flops=2 * rows * width * half * len(weights),
+            transcendentals=rows * half if has_first else 0,
+            bytes_accessed=2 * width * half * len(weights) + 4 * rows * width,
         ),
         name="experts",
-    )(own, other, in_hbm(w_first), in_hbm(w_second))
+    )(source, *weights)
 
 
 def combine_kernel(after_out, mod, pick0, pick1, prob, back, result_out, after, last, result, sem, sems):
@@ -285,7 +307,8 @@
     tok_rows, width = tokens.shape
     mod = modulation.reshape(6, width)
     pieces = jnp.concatenate([w_query, w_key, w_value, w_out.T], axis=1)
-    weights = lax.all_gather(pieces, ("grp", "dev"), axis=0, tiled=True)
+    weights = lax.all_gather(pieces, ("dev", "grp"), axis=0, tiled=True)
+    weights = weights.reshape(lax.axis_size("dev"), lax.axis_size("grp"), *pieces.shape)
 
     xn = (normalize(tokens.astype(F32)) * (1.0 + mod[1:2]) + mod[0:1]).astype(BF16)
     experts = lax.axis_size("dev")
@@ -309,8 +332,14 @@
     w_first, w_second = w_in[0], w_back[0]
 
     own = shuffle(send)
-    mine, theirs = expert_half(own, lax.ppermute(own, "grp", swap), w_first, w_second)
-    back = shuffle(add(mine, lax.ppermute(theirs, "grp", swap)))
+    other = lax.ppermute(own, "grp", swap)
+    hidden = expert_rows(own, rows, w_first=w_first)
+    other, hidden = lax.optimization_barrier((other, hidden))
+    theirs = expert_rows(other, rows, w_first=w_first, w_second=w_second)
+    hidden, theirs = lax.optimization_barrier((hidden, theirs))
+    arrived = lax.ppermute(theirs, "grp", swap)
+    mine = expert_rows(hidden, rows, w_second=w_second)
+    back = shuffle(add(mine, arrived))
     return combine(after, mod, picks[0], picks[1], route_prob, back)
 
 

time: 238 us -> 233 us (0.979)
  waiting for transfers between devices: 122 us -> 112 us
  Pallas kernels: 41.4 us -> 46.4 us
    ppermute x2, waiting for transfers between devices: 9.68 us -> 0.01 us  [the longest x1 0.01 us: body(): other = lax.ppermute(own, 'grp', swap)]
    pallas_call x1 -> x3, Pallas kernels: 27.5 us -> 32.4 us  [expert_rows(): pl.pallas_call(functools.partial(experts_kernel, has_first, has_second),...]
  transfers between devices with their start and end apart: 4 -> 4, of which waited for: 4 -> 2; matrix products, arithmetic and copies ran while one was open for 3% -> 3% of each run, Pallas kernels for 0% -> 7%
where the time goes in v4:
time: 233 us
  waiting for transfers between devices  112 us (48%)
  Pallas kernels  46.4 us (20%)
  blocking collectives  43.4 us (19%)
  between operations  13.6 us (6%)
  other arithmetic  9.44 us (4%)
  starting transfers between devices  6.53 us (3%)
    all_gather x1, waiting for transfers between devices, body(): weights = lax.all_gather(pieces, ('dev', 'grp'), axis=0, tiled=True)  78.9 us
    all_to_all x1, blocking collectives, shuffle(): lax.all_to_all(folded, 'dev', split_axis=0, concat_axis=0, tiled=True, ax...  43.4 us
    all_to_all x1, waiting for transfers between devices, shuffle(): lax.all_to_all(folded, 'dev', split_axis=0, concat_axis=0, tiled=True, ax...  33.4 us
    pallas_call x3, Pallas kernels, expert_rows(): pl.pallas_call(functools.partial(experts_kernel, has_first, has_second),...  32.4 us
    pallas_call x1, Pallas kernels, attention(): pl.pallas_call(attention_kernel, in_specs=[vmem] * 4 + [pl.BlockSpec(memo...  10.2 us
    all_to_all x1, starting transfers between devices, shuffle(): lax.all_to_all(folded, 'dev', split_axis=0, concat_axis=0, tiled=True, ax...  5.95 us
  transfers between devices with their start and end apart: 4, of which 2 were waited for; matrix products, arithmetic and copies ran while one was open for 3% of the time, Pallas kernels for 7%

profile of v4, /device:TPU:0, one launch (start us, length us, event | category | flops | bytes accessed | tf_op | source)
XLA Modules:
  0.0 232.6 jit_solution(17792036578293311272)
XLA Ops:
  6.5 1.6 pad_maximum_fusion
  8.1 0.0 all-gather.2.cloned.1.call-update
  8.1 0.5 broadcast.162
  8.7 1.5 reduce.3
  10.2 0.7 fusion.24
  10.9 0.2 select_reduce_fusion.1
  11.2 1.4 convert_reduce_fusion
  12.6 0.4 fusion.3
  13.1 0.2 fusion.11.sel
  13.2 0.7 slice_add_fusion
  14.0 0.5 fusion.6.xn
  14.4 78.9 %all-gather.2.cloned.1.call-done = bf16[2048,4096]{1,0:T(8,128)(2,1)} async-done(((bf16[16,4096]{1,0:T(8,128)(2,1)}), bf16[2048,4096]{1,0:T(8,128)(2,1)}) %all-gather.2.cloned.1.call-update) | async-done | bytes 16777232 | tf_op jit(solution)/shard_map/all_gather | solution.py:310
  93.3 10.2 %attention.1 = (f32[256,2048]{1,0:T(8,128)}, bf16[512,2560]{1,0:T(8,128)(2,1)S(1)}) custom-call(bf16[256,2048]{1,0:T(8,128)(2,1)S(1)} %fusion.6.xn, bf16[256,2048]{1,0:T(8,128)(2,1)S(1)} %copy-done, f32[6,2048]{1,0:T(8,128)S(1)} %reshape.98.mod, bf16[640,256]{1,0:T(8,128)(2,1)S(1)} %fusion.11.sel, bf16[64,2,16,4096]{3,2,1,0:T(8,128)(2,1)} %bitcast.32), custom_call_target="tpu_custom_call" | custom-call | flops 7000000000 | bytes 24000000 | tf_op jit(solution)/shard_map/attention/pallas_call | solution.py:128
  103.5 43.4 %all_to_all.10 = bf16[64,8,2560]{2,1,0:T(8,128)(2,1)S(1)} all-to-all(bf16[64,8,2560]{2,1,0:T(8,128)(2,1)S(1)} %bitcast.18), channel_id=1, replica_groups={{0,21,42,63,4,25,46,51,8,29,34,55,12,17,38,59,1,22,43,60,5,26,47,48,9,3..., dimensions={0} | all-to-all | bytes 5242880 | tf_op jit(solution)/shard_map/all_to_all | solution.py:327
  146.9 9.0 %experts.3.refs_0_ = bf16[640,2048]{1,0:T(8,128)(2,1)S(1)} custom-call(bf16[512,2560]{1,0:T(8,128)(2,1)S(1)} %bitcast.20, bf16[2048,2048]{1,0:T(8,128)(2,1)} %bitcast.33), custom_call_target="tpu_custom_call" | custom-call | flops 5368709120 | bytes 13631488 | tf_op jit(solution)/shard_map/experts/pallas_call | solution.py:212
  155.9 15.4 %experts.4 = bf16[512,2560]{1,0:T(8,128)(2,1)S(1)} custom-call(bf16[512,2560]{1,0:T(8,128)(2,1)S(1)} %collective-permute-done.refs_0_, bf16[2048,2048]{1,0:T(8,128)(2,1)} %bitcast.34, bf16[2048,2048]{1,0:T(8,128)(2,1)} %bitcast.35), custom_call_target="tpu_custom_call" | custom-call | flops 10737418240 | bytes 22020096 | tf_op jit(solution)/shard_map/experts/pallas_call | solution.py:212
  171.3 0.6 collective-permute-start.1
  171.9 8.1 %experts.5 = bf16[512,2560]{1,0:T(8,128)(2,1)S(1)} custom-call(bf16[640,2048]{1,0:T(8,128)(2,1)S(1)} %experts.3.refs_0_, bf16[2048,2048]{1,0:T(8,128)(2,1)} %bitcast.36), custom_call_target="tpu_custom_call" | custom-call | flops 5368709120 | bytes 13631488 | tf_op jit(solution)/shard_map/experts/pallas_call | solution.py:212
  180.0 2.2 fusion
  182.1 6.0 %all-to-all-start.1 = ((bf16[64,8,2560]{2,1,0:T(8,128)(2,1)}), bf16[64,8,2560]{2,1,0:T(8,128)(2,1)S(1)}, u32[]{:S(2)}, u32[]{:S(2)}) async-start(bf16[64,8,2560]{2,1,0:T(8,128)(2,1)} %fusion), calls=%async_computation.1 | async-start | bytes 5242880 | tf_op jit(solution)/shard_map/all_to_all | solution.py:327
  188.1 0.1 copy.11.prob
  188.3 0.2 fusion.9
  188.5 33.4 %all-to-all-done.1 = bf16[64,8,2560]{2,1,0:T(8,128)(2,1)S(1)} async-done(((bf16[64,8,2560]{2,1,0:T(8,128)(2,1)}), bf16[64,8,2560]{2,1,0:T(8,128)(2,1)S(1)}, u32[]{:S(2)}, u32[]{:S(2)}) %all-to-all-start.1) | async-done | bytes 2621472 | tf_op jit(solution)/shard_map/all_to_all | solution.py:327
  221.9 3.8 %combine.1 = bf16[256,2048]{1,0:T(8,128)(2,1)} custom-call(f32[256,2048]{1,0:T(8,128)} %get-tuple-element.11.after_out, f32[6,2048]{1,0:T(8,128)S(1)} %reshape.98.mod, bf16[256,640]{1,0:T(8,128)(2,1)S(1)} %get-tuple-element.27.pick0, bf16[256,640]{1,0:T(8,128)(2,1)S(1)} %get-tuple-element.28.pick1, f32[256,2]{1,0:T(8,128)S(1)} %copy.11.prob, ...), custom_call_target="tpu_custom_call" | custom-call | flops 3000000000 | bytes 7000000 | tf_op jit(solution)/shard_map/combine/pallas_call | solution.py:260
  (16 shorter events, 0.1 us)
Async XLA Ops:
  6.5 6.1 %copy-start = (bf16[256,2048]{1,0:T(8,128)(2,1)S(1)}, bf16[256,2048]{1,0:T(8,128)(2,1)}, u32[]{:S(2)}) copy-start(bf16[256,2048]{1,0:T(8,128)(2,1)} %tok.1) | copy-start | bytes 3145732
  6.5 86.8 %all-gather.2.cloned.1.call-start = ((), (), s32[]{:S(2)}) async-start(), calls=%async_computation.2 | async-start | bytes 16908288 | tf_op jit(solution)/shard_map/all_gather | solution.py:310
  146.9 9.0 %collective-permute-start = (bf16[512,2560]{1,0:T(8,128)(2,1)S(1)}, bf16[512,2560]{1,0:T(8,128)(2,1)S(1)}, u32[]{:S(2)}, u32[]{:S(2)}) collective-permute-start(bf16[512,2560]{1,0:T(8,128)(2,1)S(1)} %bitcast.19), channel_id=1, source_target_pairs={{0,64},{64,0},{1,65},{65,1},{2,66},{66,2},{3,67},{67,3},{4,68},{68... | collective-permute-start | bytes 7864328 | tf_op jit(solution)/shard_map/ppermute | solution.py:335
  171.3 8.7 %collective-permute-start.1 = (bf16[512,2560]{1,0:T(8,128)(2,1)S(1)}, bf16[512,2560]{1,0:T(8,128)(2,1)S(1)}, u32[]{:S(2)}, u32[]{:S(2)}) collective-permute-start(bf16[512,2560]{1,0:T(8,128)(2,1)S(1)} %experts.4), channel_id=1, source_target_pairs={{0,64},{64,0},{1,65},{65,1},{2,66},{66,2},{3,67},{67,3},{4,68},{68... | collective-permute-start | bytes 7864328 | tf_op jit(solution)/shard_map/ppermute | solution.py:340
  182.1 6.0 %copy-start.1 = (f32[256,2]{0,1:T(2,128)S(1)}, f32[256,2]{0,1:T(2,128)}, u32[]{:S(2)}) copy-start(f32[256,2]{0,1:T(2,128)} %param.19) | copy-start | bytes 6148
  182.1 39.8 %all-to-all-start.1 = ((bf16[64,8,2560]{2,1,0:T(8,128)(2,1)}), bf16[64,8,2560]{2,1,0:T(8,128)(2,1)S(1)}, u32[]{:S(2)}, u32[]{:S(2)}) async-start(bf16[64,8,2560]{2,1,0:T(8,128)(2,1)} %fusion), calls=%async_computation.1 | async-start | bytes 5242880 | tf_op jit(solution)/shard_map/all_to_all | solution.py:327
Sparse Core Ops, SparseCore 0:
  10.5 82.7 all-gather.1

commit v5 on v4

--- a/solution.py
+++ b/solution.py
@@ -230,6 +230,25 @@
     )(source, *weights)
 
 
+def add_kernel(a, b, total):
+    total[...] = (a[...].astype(F32) + b[...].astype(F32)).astype(BF16)
+
+
+def add_rows(a, b):
+    vmem = pl.BlockSpec(memory_space=pltpu.VMEM)
+    return pl.pallas_call(
+        add_kernel,
+        in_specs=[vmem] * 2,
+        out_specs=vmem,
+        out_shape=jax.ShapeDtypeStruct(a.shape, BF16),
+        compiler_params=pltpu.CompilerParams(vmem_limit_bytes=4 * MIB),
+        cost_estimate=pl.CostEstimate(
+            flops=a.size, transcendentals=0, bytes_accessed=6 * a.size
+        ),
+        name="add",
+    )(a, b)
+
+
 def combine_kernel(after_out, mod, pick0, pick1, prob, back, result_out, after, last, result, sem, sems):
     kept = pltpu.make_async_copy(after_out, after, sem)
     kept.start()
@@ -328,7 +347,6 @@
             folded, "dev", split_axis=0, concat_axis=0, tiled=True, axis_index_groups=groups
         ).reshape(rows.shape)
 
-    add = lambda a, b: (a.astype(F32) + b.astype(F32)).astype(BF16)
     w_first, w_second = w_in[0], w_back[0]
 
     own = shuffle(send)
@@ -339,7 +357,7 @@
     hidden, theirs = lax.optimization_barrier((hidden, theirs))
     arrived = lax.ppermute(theirs, "grp", swap)
     mine = expert_rows(hidden, rows, w_second=w_second)
-    back = shuffle(add(mine, arrived))
+    back = shuffle(add_rows(mine, arrived))
     return combine(after, mod, picks[0], picks[1], route_prob, back)
 
 

time: 233 us -> 233 us (level)
  no operation moved by 1% of the time
where the time goes in v5:
time: 233 us; the launch traced here: 232 us
  waiting for transfers between devices  112 us (48%)
  Pallas kernels  48.5 us (21%)
  blocking collectives  43.4 us (19%)
  between operations  13.6 us (6%)
  other arithmetic  7.25 us (3%)
  starting transfers between devices  6.53 us (3%)
    all_gather x1, waiting for transfers between devices, body(): weights = lax.all_gather(pieces, ('dev', 'grp'), axis=0, tiled=True)  78.9 us
    all_to_all x1, blocking collectives, shuffle(): lax.all_to_all(folded, 'dev', split_axis=0, concat_axis=0, tiled=True, ax...  43.4 us
    all_to_all x1, waiting for transfers between devices, shuffle(): lax.all_to_all(folded, 'dev', split_axis=0, concat_axis=0, tiled=True, ax...  33.4 us
    pallas_call x3, Pallas kernels, expert_rows(): pl.pallas_call(functools.partial(experts_kernel, has_first, has_second),...  32.4 us
    pallas_call x1, Pallas kernels, attention(): pl.pallas_call(attention_kernel, in_specs=[vmem] * 4 + [pl.BlockSpec(memo...  10.2 us
    all_to_all x1, starting transfers between devices, shuffle(): lax.all_to_all(folded, 'dev', split_axis=0, concat_axis=0, tiled=True, ax...  5.96 us
  transfers between devices with their start and end apart: 4, of which 2 were waited for; matrix products, arithmetic and copies ran while one was open for 3% of the time, Pallas kernels for 7%

profile of v5, /device:TPU:0, one launch (start us, length us, event | category | flops | bytes accessed | tf_op | source)
XLA Modules:
  0.0 232.5 jit_solution(355691297157604982)
XLA Ops:
  6.5 1.6 pad_maximum_fusion
  8.1 0.0 all-gather.2.cloned.1.call-update
  8.1 0.5 broadcast.162
  8.7 1.5 reduce.3
  10.2 0.7 fusion.23
  10.9 0.2 select_reduce_fusion.1
  11.2 1.4 convert_reduce_fusion
  12.6 0.4 fusion.2
  13.1 0.2 fusion.10.sel
  13.2 0.7 slice_add_fusion
  14.0 0.5 fusion.5.xn
  14.4 78.9 %all-gather.2.cloned.1.call-done = bf16[2048,4096]{1,0:T(8,128)(2,1)} async-done(((bf16[16,4096]{1,0:T(8,128)(2,1)}), bf16[2048,4096]{1,0:T(8,128)(2,1)}) %all-gather.2.cloned.1.call-update) | async-done | bytes 16777232 | tf_op jit(solution)/shard_map/all_gather | solution.py:329
  93.3 10.2 %attention.1 = (f32[256,2048]{1,0:T(8,128)}, bf16[512,2560]{1,0:T(8,128)(2,1)S(1)}) custom-call(bf16[256,2048]{1,0:T(8,128)(2,1)S(1)} %fusion.5.xn, bf16[256,2048]{1,0:T(8,128)(2,1)S(1)} %copy-done, f32[6,2048]{1,0:T(8,128)S(1)} %reshape.98.mod, bf16[640,256]{1,0:T(8,128)(2,1)S(1)} %fusion.10.sel, bf16[64,2,16,4096]{3,2,1,0:T(8,128)(2,1)} %bitcast.31), custom_call_target="tpu_custom_call" | custom-call | flops 7000000000 | bytes 24000000 | tf_op jit(solution)/shard_map/attention/pallas_call | solution.py:128
  103.5 43.4 %all_to_all.10 = bf16[64,8,2560]{2,1,0:T(8,128)(2,1)S(1)} all-to-all(bf16[64,8,2560]{2,1,0:T(8,128)(2,1)S(1)} %bitcast.17), channel_id=1, replica_groups={{0,21,42,63,4,25,46,51,8,29,34,55,12,17,38,59,1,22,43,60,5,26,47,48,9,3..., dimensions={0} | all-to-all | bytes 5242880 | tf_op jit(solution)/shard_map/all_to_all | solution.py:346
  146.9 9.0 %experts.3.refs_0_ = bf16[640,2048]{1,0:T(8,128)(2,1)S(1)} custom-call(bf16[512,2560]{1,0:T(8,128)(2,1)S(1)} %bitcast.19, bf16[2048,2048]{1,0:T(8,128)(2,1)} %bitcast.32), custom_call_target="tpu_custom_call" | custom-call | flops 5368709120 | bytes 13631488 | tf_op jit(solution)/shard_map/experts/pallas_call | solution.py:212
  155.9 15.4 %experts.4 = bf16[512,2560]{1,0:T(8,128)(2,1)S(1)} custom-call(bf16[512,2560]{1,0:T(8,128)(2,1)S(1)} %collective-permute-done.refs_0_, bf16[2048,2048]{1,0:T(8,128)(2,1)} %bitcast.33, bf16[2048,2048]{1,0:T(8,128)(2,1)} %bitcast.34), custom_call_target="tpu_custom_call" | custom-call | flops 10737418240 | bytes 22020096 | tf_op jit(solution)/shard_map/experts/pallas_call | solution.py:212
  171.3 0.6 collective-permute-start.1
  171.9 8.0 %experts.5.a = bf16[512,2560]{1,0:T(8,128)(2,1)S(1)} custom-call(bf16[640,2048]{1,0:T(8,128)(2,1)S(1)} %experts.3.refs_0_, bf16[2048,2048]{1,0:T(8,128)(2,1)} %bitcast.35), custom_call_target="tpu_custom_call" | custom-call | flops 5368709120 | bytes 13631488 | tf_op jit(solution)/shard_map/experts/pallas_call | solution.py:212
  179.9 2.1 add.216
  182.0 6.0 %all-to-all-start.1 = ((bf16[64,8,2560]{2,1,0:T(8,128)(2,1)}), bf16[64,8,2560]{2,1,0:T(8,128)(2,1)S(1)}, u32[]{:S(2)}, u32[]{:S(2)}) async-start(bf16[64,8,2560]{2,1,0:T(8,128)(2,1)} %bitcast.14), calls=%async_computation.1 | async-start | bytes 5242880 | tf_op jit(solution)/shard_map/all_to_all | solution.py:346
  188.0 0.1 copy.11.prob
  188.2 0.2 fusion.8
  188.4 33.4 %all-to-all-done.1 = bf16[64,8,2560]{2,1,0:T(8,128)(2,1)S(1)} async-done(((bf16[64,8,2560]{2,1,0:T(8,128)(2,1)}), bf16[64,8,2560]{2,1,0:T(8,128)(2,1)S(1)}, u32[]{:S(2)}, u32[]{:S(2)}) %all-to-all-start.1) | async-done | bytes 2621472 | tf_op jit(solution)/shard_map/all_to_all | solution.py:346
  221.8 3.8 %combine.1 = bf16[256,2048]{1,0:T(8,128)(2,1)} custom-call(f32[256,2048]{1,0:T(8,128)} %get-tuple-element.11.after_out, f32[6,2048]{1,0:T(8,128)S(1)} %reshape.98.mod, bf16[256,640]{1,0:T(8,128)(2,1)S(1)} %get-tuple-element.27.pick0, bf16[256,640]{1,0:T(8,128)(2,1)S(1)} %get-tuple-element.28.pick1, f32[256,2]{1,0:T(8,128)S(1)} %copy.11.prob, ...), custom_call_target="tpu_custom_call" | custom-call | flops 3000000000 | bytes 7000000 | tf_op jit(solution)/shard_map/combine/pallas_call | solution.py:279
  (16 shorter events, 0.1 us)
Async XLA Ops:
  6.5 6.1 %copy-start = (bf16[256,2048]{1,0:T(8,128)(2,1)S(1)}, bf16[256,2048]{1,0:T(8,128)(2,1)}, u32[]{:S(2)}) copy-start(bf16[256,2048]{1,0:T(8,128)(2,1)} %tok.1) | copy-start | bytes 3145732
  6.5 86.8 %all-gather.2.cloned.1.call-start = ((), (), s32[]{:S(2)}) async-start(), calls=%async_computation.2 | async-start | bytes 16908288 | tf_op jit(solution)/shard_map/all_gather | solution.py:329
  146.9 9.0 %collective-permute-start = (bf16[512,2560]{1,0:T(8,128)(2,1)S(1)}, bf16[512,2560]{1,0:T(8,128)(2,1)S(1)}, u32[]{:S(2)}, u32[]{:S(2)}) collective-permute-start(bf16[512,2560]{1,0:T(8,128)(2,1)S(1)} %bitcast.18), channel_id=1, source_target_pairs={{0,64},{64,0},{1,65},{65,1},{2,66},{66,2},{3,67},{67,3},{4,68},{68... | collective-permute-start | bytes 7864328 | tf_op jit(solution)/shard_map/ppermute | solution.py:353
  171.3 8.6 %collective-permute-start.1 = (bf16[512,2560]{1,0:T(8,128)(2,1)S(1)}, bf16[512,2560]{1,0:T(8,128)(2,1)S(1)}, u32[]{:S(2)}, u32[]{:S(2)}) collective-permute-start(bf16[512,2560]{1,0:T(8,128)(2,1)S(1)} %experts.4), channel_id=1, source_target_pairs={{0,64},{64,0},{1,65},{65,1},{2,66},{66,2},{3,67},{67,3},{4,68},{68... | collective-permute-start | bytes 7864328 | tf_op jit(solution)/shard_map/ppermute | solution.py:358
  182.0 6.0 %copy-start.1 = (f32[256,2]{0,1:T(2,128)S(1)}, f32[256,2]{0,1:T(2,128)}, u32[]{:S(2)}) copy-start(f32[256,2]{0,1:T(2,128)} %param.19) | copy-start | bytes 6148
  182.0 39.8 %all-to-all-start.1 = ((bf16[64,8,2560]{2,1,0:T(8,128)(2,1)}), bf16[64,8,2560]{2,1,0:T(8,128)(2,1)S(1)}, u32[]{:S(2)}, u32[]{:S(2)}) async-start(bf16[64,8,2560]{2,1,0:T(8,128)(2,1)} %bitcast.14), calls=%async_computation.1 | async-start | bytes 5242880 | tf_op jit(solution)/shard_map/all_to_all | solution.py:346
Sparse Core Ops, SparseCore 0:
  10.5 82.7 all-gather.1
